TPU v7x, 256 devices: a whole 4x4x8 slice. The times are simulated.
256 devices in a mesh: band: 8 (over z), ord: 32 (over x, y, core).
Axes of the slice: x: 4, y: 4, z: 8, core: 2. Of those that a mesh axis runs over, the one named last changes fastest.
Arguments:
- density: bfloat16 [8, 128, 256, 512], P('band', None, 'ord'), may hold values from -6 to 6
- degree_weights: float32 [8, 256], P('band'), may hold values from 0.25 to 1
- row_orders: int32 [256], replicated, may hold values from 0 to 255, each once
- target_cycles: int32 [128], replicated, may hold values from 0 to 255, as said below
Outputs:
- coeffs: bfloat16 [8, 256, 128, 2, 256], P('band', 'ord')
- potential: float32 [128, 128, 512], P('band', 'ord')
Inputs may be any that keep to these rules, and one draw needn't show every extreme that they name: `row_orders`: each order appears once. `target_cycles`: 128 distinct cycle indices.
All inputs are finite; a program needn't handle non-finite values.
Results may differ from a plain program's by a relative error of at most 0.0095.
Values may be sent and summed in bfloat16 or wider, within the bound.
No kernel may reach another device: no remote copies, remote signals or barrier semaphores. Data moves between devices by JAX's collectives and lax.ppermute only.
A program may use at most 64 MiB of HBM per device.

v0:
```python
import math

import jax
import jax.numpy as jnp
from jax import lax
from jax.sharding import PartitionSpec as P


def cycle_grid(cycle_count):
    centers = (jnp.arange(cycle_count, dtype=jnp.float32) + 0.5) * (math.pi / cycle_count)
    return (jnp.cos(centers), jnp.sin(centers))


def legendre_rows(order_vals, cycle_count, degree_count):
    cosines, sine_vals = cycle_grid(cycle_count)
    steps_f = jnp.arange(1, degree_count, dtype=jnp.float32)
    log_terms = jnp.log((2.0 * steps_f + 1.0) / (2.0 * steps_f))
    gamma_terms = jnp.sum(
        jnp.where(steps_f[None, :] <= order_vals[:, None], log_terms[None, :], 0.0), axis=1
    )
    log_start = (
        0.5 * (math.log(1.0 / (4.0 * math.pi)) + gamma_terms)[:, None]
        + order_vals[:, None] * jnp.log(sine_vals)[None, :]
    )
    shift_vals = jnp.clip(-log_start - 40.0, 0.0, 80.0)
    sectoral_terms = jnp.exp(log_start + shift_vals)
    orders_col = order_vals[:, None]

    def advance(carry, degree_f):
        previous, earlier = carry
        denom = jnp.maximum(degree_f * degree_f - orders_col * orders_col, 1.0)
        growth = jnp.sqrt(jnp.maximum(4.0 * degree_f * degree_f - 1.0, 0.0) / denom)
        lower = degree_f - 1.0
        damping = jnp.sqrt(
            jnp.maximum(lower * lower - orders_col * orders_col, 0.0)
            / jnp.maximum(4.0 * lower * lower - 1.0, 1.0)
        )
        grown = growth * (cosines[None, :] * previous - damping * earlier)
        current = jnp.where(
            degree_f < orders_col, 0.0, jnp.where(degree_f == orders_col, sectoral_terms, grown)
        )
        return ((current, previous), current)

    empty = jnp.zeros(sectoral_terms.shape, jnp.float32)
    _, table = lax.scan(advance, (empty, empty), jnp.arange(degree_count, dtype=jnp.float32))
    return table * jnp.exp(-shift_vals)[None, :, :]


def forward_table(orders, lon_count, lat_count):
    lon_index = jnp.arange(lon_count, dtype=jnp.int32)
    turns = lon_index[:, None] * orders[None, :] % lon_count
    phases = turns.astype(jnp.float32) * (2.0 * math.pi / lon_count)
    factor = 2.0 * math.pi / lon_count * math.sqrt(lat_count * lon_count / (4.0 * math.pi))
    return jnp.stack([factor * jnp.cos(phases), -factor * jnp.sin(phases)], axis=1).astype(
        jnp.bfloat16
    )


def inverse_table(orders, lon_count, lat_count):
    lon_index = jnp.arange(lon_count, dtype=jnp.int32)
    turns = orders[:, None] * lon_index[None, :] % lon_count
    phases = turns.astype(jnp.float32) * (2.0 * math.pi / lon_count)
    factor = jnp.where(orders == 0, 1.0, 2.0).astype(jnp.float32)[:, None] / math.sqrt(
        lat_count * lon_count / (4.0 * math.pi)
    )
    return jnp.stack([factor * jnp.cos(phases), -factor * jnp.sin(phases)], axis=1).astype(
        jnp.bfloat16
    )


def local(density, degree_weights, row_orders, target_cycles):
    ord_count = lax.axis_size("ord")
    ord_index = lax.axis_index("ord")
    dens_count = density.shape[1]
    cycle_count = density.shape[2] * ord_count
    lon_count = density.shape[3]
    degree_count = degree_weights.shape[1]
    per_device = degree_count // ord_count
    own_cycles = density.shape[2]
    forward = forward_table(row_orders, lon_count, cycle_count)
    spectra = jnp.einsum(
        "qrk,kci->irqc", density[0], forward, preferred_element_type=jnp.float32
    ).astype(jnp.bfloat16)
    spectra = spectra.reshape(degree_count, own_cycles, dens_count * 2)
    by_order = lax.all_to_all(spectra, "ord", split_axis=0, concat_axis=1, tiled=True)
    by_order = by_order.reshape(per_device, cycle_count, dens_count, 2)
    local_orders = lax.dynamic_slice_in_dim(row_orders, ord_index * per_device, per_device)
    cosines, sine_vals = cycle_grid(cycle_count)
    legendre = legendre_rows(local_orders.astype(jnp.float32), cycle_count, degree_count)
    analysis = (legendre * (math.pi / cycle_count * sine_vals)[None, None, :]).astype(jnp.bfloat16)
    coeffs = jnp.einsum(
        "ijqc,lij->iqcl", by_order, analysis, preferred_element_type=jnp.float32
    ).astype(jnp.bfloat16)
    scaled_values = (coeffs.astype(jnp.float32) * degree_weights[0][None, None, None, :]).astype(
        jnp.bfloat16
    )
    synthesis_result = legendre.astype(jnp.bfloat16)
    cycle_modes = jnp.einsum(
        "iqcl,lir->iqcr", scaled_values, synthesis_result, preferred_element_type=jnp.float32
    ).astype(jnp.bfloat16)
    arrived = lax.all_to_all(cycle_modes, "ord", split_axis=1, concat_axis=0, tiled=True)
    gathered = jnp.take(arrived, target_cycles, axis=3)
    inverse = inverse_table(row_orders, lon_count, cycle_count)
    potential = lax.psum_scatter(
        jnp.einsum("iqcr,ick->rqk", gathered, inverse, preferred_element_type=jnp.float32),
        "band",
        scatter_dimension=0,
        tiled=True,
    )
    return (coeffs[None], potential)


def solution(mesh):
    in_specs = (P("band", None, "ord", None), P("band", None), P(), P())
    out_specs = (P("band", "ord", None, None, None), P("band", "ord", None))
    return jax.shard_map(local, mesh=mesh, in_specs=in_specs, out_specs=out_specs, check_vma=False)
```

profile of v0, /device:TPU:1, one launch (start us, length us, event | category | flops | bytes accessed | tf_op | source)
XLA Modules:
  0.0 1378.4 jit_solution(3919413770137926248)
XLA Ops:
  7.2 3.0 multiply_convert_fusion.7
  10.1 1.9 fusion.5
  12.7 2.1 copy.78
  14.7 8.6 all-to-all-start
  23.7 1193.2 %while.18 = (s32[]{:T(128)}, f32[8,256]{1,0:T(8,128)S(1)}, f32[8,256]{1,0:T(8,128)S(1)}, f32[256,8,256]{2,1,0:T(8,128)S(1)}, f32[256]{0:T(256)S(1)}, /*index=5*/...) while((s32[]{:T(128)}, f32[8,256]{1,0:T(8,128)S(1)}, ...), condition=%wide.region_2.3_spmd.clone, body=%wide.region_1.2_spmd.clone.sunk | while | flops 27214 | bytes 47575 | solution.py:45
  36.9 0.7 compare_bitcast_fusion.3
  50.9 0.7 compare_bitcast_fusion.3
  74.2 0.7 compare_bitcast_fusion.3
  88.2 0.7 compare_bitcast_fusion.3
  111.5 0.7 compare_bitcast_fusion.3
  1217.1 1.6 fusion.6
  1218.7 22.6 %copy.79 = bf16[8,32,8,256]{2,1,0,3:T(8,128)(2,1)} copy(bf16[8,32,8,256]{3,2,0,1:T(8,128)(2,1)S(1)} %bitcast.64) | data formatting | bytes 2097152 | tf_op jit(solution)/shard_map/all_to_all | solution.py:85
  1241.3 24.0 %reshape.384 = bf16[8,256,128,2]{1,0,3,2:T(8,128)(2,1)S(1)} reshape(bf16[8,32,8,256]{2,1,0,3:T(8,128)(2,1)} %copy.79) | data formatting | bytes 2097152 | tf_op jit(solution)/shard_map/reshape | solution.py:86
  1267.1 2.0 copy.83
  1269.1 7.4 all-to-all-start.1
  1276.8 2.9 multiply_convert_fusion.5
  1279.7 13.7 all-to-all-done.1
  1293.7 1.1 copy.86
  1294.8 1.0 gather_fusion
  1296.2 1.4 convolution_bitcast_fusion
  1297.6 1.4 copy.88
  1300.3 2.0 copy.89
  1302.4 67.6 %all-reduce.3.cloned.1.call-done = f32[128,4,512]{2,1,0:T(4,128)} async-done(((f32[128,4,512]{2,1,0:T(4,128)}), f32[128,4,512]{2,1,0:T(4,128)}) %all-reduce.3.cloned.1.call-update) | async-done | bytes 1048592
  1370.0 1.6 constant_dynamic-slice_fusion
  (1312 shorter events, 356.1 us)
Async XLA Ops:
  12.7 10.8 copy-start.2
  14.7 1204.0 %all-to-all-start = ((bf16[256,8,256]{2,1,0:T(8,128)(2,1)}), bf16[256,8,256]{2,1,0:T(8,128)(2,1)S(1)}, u32[]{:S(2)}, u32[]{:S(2)}) async-start(bf16[256,8,256]{2,1,0:T(8,128)(2,1)} %copy.78), calls=%async_computation | async-start | bytes 2097152 | tf_op jit(solution)/shard_map/all_to_all | solution.py:85
  1241.3 24.0 %copy-start.1 = (bf16[256,8,256,1]{2,1,0,3:T(8,128)(2,1)S(1)}, bf16[256,8,256,1]{2,1,0,3:T(8,128)(2,1)}, u32[]{:S(2)}) copy-start(bf16[256,8,256,1]{2,1,0,3:T(8,128)(2,1)} %get-tuple-element.222) | copy-start | bytes 3145732
  1265.3 1.2 copy-start
  1265.3 1.2 copy-start.3
  1267.0 9.7 copy-start.4
  1269.1 24.3 %all-to-all-start.1 = ((bf16[8,128,2,256]{3,2,0,1:T(2,128)(2,1)}), bf16[8,128,2,256]{3,2,0,1:T(2,128)(2,1)S(1)}, u32[]{:S(2)}, u32[]{:S(2)}) async-start(bf16[8,128,2,256]{3,2,0,1:T(2,128)(2,1)} %copy.83), calls=%async_computation.1 | async-start | bytes 2097152 | tf_op jit(solution)/shard_map/all_to_all | solution.py:101
  1276.5 93.5 %all-reduce.3.cloned.1.call-start = ((), (), s32[]{:S(2)}) async-start(), calls=%async_computation.2 | async-start | bytes 2097152
  1297.6 1.5 copy-start.5
Sparse Core Ops, SparseCore 0:
  1299.2 70.7 all-reduce.2
where the time goes:
time: 1400 us; the launch traced here: 1380 us
  loops' own time  838 us (60%)
  other arithmetic  213 us (15%)
  local copies, waits for them, and re-layouts  210 us (15%)
  waiting for transfers between devices  81.3 us (6%)
  starting transfers between devices  16.2 us (1%)
  between operations  14.9 us (1%)
    another operation x1, loops' own time, legendre_rows(): lax.scan(advance, (empty, empty), jnp.arange(degree_count, dtype=jnp.floa...  838 us
    lt x256, other arithmetic, advance(): degree_f < orders_col  167 us
    dynamic_slice x256, local copies, waits for them, and re-layouts, legendre_rows(): lax.scan(advance, (empty, empty), jnp.arange(degree_count, dtype=jnp.floa...  150 us
    unnamed x2, waiting for transfers between devices  67.6 us
  transfers between devices with their start and end apart: 3, of which 2 were waited for; matrix products, arithmetic and copies ran while one was open for 26% of the time, Pallas kernels for 0%

commit v1 on v0

v1 whole, which is shorter than its diff:
```python
import math

import numpy as np
import jax
import jax.numpy as jnp
from jax import lax
from jax.experimental import pallas as pl
from jax.experimental.pallas import tpu as pltpu
from jax.sharding import PartitionSpec as P

F32 = jnp.float32
BF16 = jnp.bfloat16
NN = (((1,), (0,)), ((), ()))
NT = (((1,), (1,)), ((), ()))
TN = (((0,), (0,)), ((), ()))


def dot(a, b, dims=NN):
    return lax.dot_general(a, b, dims, preferred_element_type=F32)


def trig_tables(order_count, lon_count, lat_count):
    turns = np.arange(order_count)[:, None] * np.arange(lon_count)[None, :] % lon_count
    phases = turns * (2.0 * math.pi / lon_count)
    gain = math.sqrt(lat_count * lon_count / (4.0 * math.pi))
    waves = np.concatenate([np.cos(phases), -np.sin(phases)], axis=1)
    forward = waves * (2.0 * math.pi / lon_count * gain)
    twice = np.where(np.arange(order_count) == 0, 1.0, 2.0)[:, None]
    inverse = waves * twice / gain
    kind = jnp.dtype(BF16)
    return forward.astype(np.float32).astype(kind), inverse.astype(np.float32).astype(kind)


def iota(shape, axis):
    return lax.broadcasted_iota(jnp.int32, shape, axis)


def one_hot(hit):
    return jnp.where(hit, 1.0, 0.0).astype(BF16)


def swap_matrix(outer, inner):
    n = outer * inner
    row, col = iota((n, n), 0), iota((n, n), 1)
    return one_hot(col == (row % inner) * outer + row // inner)


def forward_kernel(orders_ref, density_ref, table_ref, out_ref, turned_ref):
    picks = one_hot(iota((256, 256), 0) == orders_ref[...])
    rows = dot(picks, table_ref[...], TN)
    cos_rows = rows[:, :512].reshape(32, 8, 512)
    sin_rows = rows[:, 512:].reshape(32, 8, 512)
    forward = jnp.stack([cos_rows, sin_rows], axis=1).reshape(512, 512).astype(BF16)
    swap = swap_matrix(8, 32)
    for b in range(4):
        part = dot(swap, density_ref[b * 256 : (b + 1) * 256, :]).astype(BF16)
        turned_ref[:, b * 32 : (b + 1) * 32, :] = part.reshape(8, 32, 512)
    for j in range(0, 8, 2):
        lanes = turned_ref[j : j + 2].reshape(256, 512)
        part = dot(forward, lanes, NT).astype(BF16)
        for h in range(2):
            block = part[:, h * 128 : (h + 1) * 128].reshape(32, 16, 128)
            out_ref[:, (j + h) * 16 : (j + h + 1) * 16, :] = block


def table_kernel(own_ref, orders_ref, target_ref, grid_ref, inverse_ref,
                 analysis_ref, synthesis_ref, inv_ref, legendre_ref, rows_ref):
    sub = iota((8, 256), 0)
    order = jnp.zeros((8, 256), F32)
    for i in range(8):
        order = jnp.where(sub == i, own_ref[i].astype(F32), order)
    cosines = jnp.broadcast_to(grid_ref[0:1, :], (8, 256))
    log_sines = jnp.log(grid_ref[1:2, :])
    weights = grid_ref[2:3, :]
    steps = iota((8, 256), 1).astype(F32)
    safe = jnp.maximum(steps, 1.0)
    log_terms = jnp.log((2.0 * safe + 1.0) / (2.0 * safe))
    counted = (steps >= 1.0) & (steps <= order)
    gamma = jnp.sum(jnp.where(counted, log_terms, 0.0), axis=1, keepdims=True)
    log_start = 0.5 * (math.log(1.0 / (4.0 * math.pi)) + gamma) + order * log_sines
    shift = jnp.clip(-log_start - 40.0, 0.0, 80.0)
    sectoral = jnp.exp(log_start + shift)
    unshift = jnp.exp(-shift)
    half = order[:, :128]
    half_sq = half * half

    def wide(a):
        return jnp.concatenate([a, a], axis=1)

    def advance(step, carry):
        previous, earlier = carry
        degree = jnp.full((8, 128), step, jnp.int32).astype(F32)
        square = degree * degree
        growth = jnp.sqrt(
            jnp.maximum(4.0 * square - 1.0, 0.0) / jnp.maximum(square - half_sq, 1.0)
        )
        lower = degree - 1.0
        low_sq = lower * lower
        damping = jnp.sqrt(
            jnp.maximum(low_sq - half_sq, 0.0) / jnp.maximum(4.0 * low_sq - 1.0, 1.0)
        )
        grown = wide(growth) * (cosines * previous - wide(damping) * earlier)
        wide_degree = wide(degree)
        current = jnp.where(
            wide_degree < order, 0.0, jnp.where(wide_degree == order, sectoral, grown)
        )
        final = current * unshift
        rows = pl.ds(pl.multiple_of(step * 8, 8), 8)
        legendre_ref[0, rows, :] = final[:, :128]
        legendre_ref[1, rows, :] = final[:, 128:]
        return current, previous

    empty = sectoral * 0.0
    lax.fori_loop(0, 256, advance, (empty, empty), unroll=8)

    hits = jnp.where(iota((256, 128), 0) == target_ref[...], 1.0, 0.0)
    picks = hits.T.astype(BF16)
    for i in range(8):
        halves = [legendre_ref[h, pl.ds(i, 256, stride=8), :] for h in range(2)]
        own = jnp.concatenate(halves, axis=1)
        analysis_ref[i] = (own * weights).astype(BF16)
        synthesis_ref[i] = dot(picks, own.astype(BF16), NT).astype(BF16)

    places = one_hot(iota((256, 256), 0) == orders_ref[...])
    rows = dot(places, inverse_ref[...], TN)
    for c in range(8):
        rows_ref[c] = rows[:, c * 128 : (c + 1) * 128]
    for i in range(8):
        for c in range(8):
            own = rows_ref[c, pl.ds(i, 32, stride=8), :].astype(BF16)
            top = i * 64 + c // 4 * 32
            inv_ref[top : top + 32, c % 4 * 128 : (c % 4 + 1) * 128] = own


def order_kernel(spectra_ref, analysis_ref, synthesis_ref, weights_ref,
                 coeffs_ref, out_ref, cycles_ref, modes_ref):
    swap = swap_matrix(16, 16)
    for b in range(0, 16, 2):
        first = spectra_ref[b * 256 : (b + 1) * 256, :]
        second = spectra_ref[(b + 1) * 256 : (b + 2) * 256, :]
        both = dot(swap, jnp.concatenate([first, second], axis=1)).astype(BF16)
        cycles_ref[:, b * 16 : (b + 1) * 16, :] = both[:, :128].reshape(16, 16, 128)
        cycles_ref[:, (b + 1) * 16 : (b + 2) * 16, :] = both[:, 128:].reshape(16, 16, 128)
    scale = jnp.broadcast_to(weights_ref[...], (128, 256)).T
    scale = jnp.concatenate([scale, scale], axis=1)
    row, col = iota((256, 256), 0), iota((256, 256), 1)
    interleave = one_hot(col == (row % 2) * 128 + row // 2)
    deal = one_hot(col == (row // 4 % 2) * 128 + row // 8 * 4 + row % 4)
    for i in range(8):
        lanes = jnp.concatenate([cycles_ref[i], cycles_ref[8 + i]], axis=1)
        harmonic = dot(analysis_ref[i], lanes).astype(BF16)
        coeffs_ref[i] = dot(interleave, harmonic, NT).astype(BF16)
        scaled = (harmonic.astype(F32) * scale).astype(BF16)
        modes = dot(synthesis_ref[i], scaled).astype(BF16)
        modes_ref[:, i * 16 : (i + 1) * 16, :] = modes.reshape(8, 16, 256)
    for b in range(8):
        block = dot(deal, modes_ref[b], NT)
        out_ref[b * 256 : (b + 1) * 256, :] = block.astype(BF16)


def inverse_kernel(modes_ref, inv_ref, out_ref, sum_ref):
    total = modes_ref[0:256, :].astype(F32)
    for g in range(1, 8):
        total = total + modes_ref[g * 256 : (g + 1) * 256, :].astype(F32)
    sum_ref[...] = total
    blocks = []
    for q in range(4):
        parts = [sum_ref[pl.ds(c * 4 + q, 32, stride=8), :] for c in range(2)]
        turned = jnp.concatenate(parts, axis=0).T
        own = [turned[i * 16 : (i + 1) * 16, :] for i in range(8)]
        blocks.append(jnp.concatenate(own, axis=1))
    left = jnp.concatenate(blocks, axis=0).astype(BF16)
    result = dot(left, inv_ref[...])
    for q in range(4):
        out_ref[:, q, :] = result[q * 16 : (q + 1) * 16, :]


def struct(shape, kind):
    return jax.ShapeDtypeStruct(shape, kind)


VMEM_SPEC = pl.BlockSpec(memory_space=pltpu.VMEM)
SMEM_SPEC = pl.BlockSpec(memory_space=pltpu.SMEM)


def local(density, degree_weights, row_orders, target_cycles):
    forward_trig, inverse_trig = trig_tables(256, 512, 256)
    orders_row = row_orders.reshape(1, 256)
    own_orders = lax.dynamic_slice_in_dim(row_orders, lax.axis_index("ord") * 8, 8)
    centers = (jnp.arange(256, dtype=F32) + 0.5) * (math.pi / 256)
    grid = jnp.stack([jnp.cos(centers), jnp.sin(centers), math.pi / 256 * jnp.sin(centers)])

    spectra = pl.pallas_call(
        forward_kernel,
        out_shape=struct((32, 128, 128), BF16),
        in_specs=[VMEM_SPEC] * 3,
        out_specs=VMEM_SPEC,
        scratch_shapes=[pltpu.VMEM((8, 128, 512), BF16)],
        name="forward",
    )(orders_row, density.reshape(1024, 512), jnp.asarray(forward_trig))
    by_order = lax.all_to_all(spectra, "ord", split_axis=0, concat_axis=0, tiled=True)

    analysis, synthesis, inverse_rows = pl.pallas_call(
        table_kernel,
        out_shape=(
            struct((8, 256, 256), BF16),
            struct((8, 128, 256), BF16),
            struct((512, 512), BF16),
        ),
        in_specs=[SMEM_SPEC] + [VMEM_SPEC] * 4,
        out_specs=(VMEM_SPEC,) * 3,
        scratch_shapes=[pltpu.VMEM((2, 2048, 128), F32), pltpu.VMEM((8, 256, 128), F32)],
        name="tables",
    )(own_orders, orders_row, target_cycles.reshape(1, 128), grid, jnp.asarray(inverse_trig))

    coeffs, modes = pl.pallas_call(
        order_kernel,
        out_shape=(struct((8, 256, 256), BF16), struct((2048, 128), BF16)),
        in_specs=[VMEM_SPEC] * 4,
        out_specs=(VMEM_SPEC,) * 2,
        scratch_shapes=[pltpu.VMEM((16, 256, 128), BF16), pltpu.VMEM((8, 128, 256), BF16)],
        name="orders",
    )(by_order.reshape(4096, 128), analysis, synthesis, degree_weights)

    arrived = lax.all_to_all(
        modes.reshape(256, 8, 128), ("band", "ord"), split_axis=0, concat_axis=0, tiled=True
    )
    potential = pl.pallas_call(
        inverse_kernel,
        out_shape=struct((16, 4, 512), F32),
        in_specs=[VMEM_SPEC] * 2,
        out_specs=VMEM_SPEC,
        scratch_shapes=[pltpu.VMEM((256, 128), F32)],
        name="inverse",
    )(arrived.reshape(2048, 128), inverse_rows)
    return coeffs.reshape(1, 8, 128, 2, 256), potential


def solution(mesh):
    in_specs = (P("band", None, "ord", None), P("band", None), P(), P())
    out_specs = (P("band", "ord", None, None, None), P("band", "ord", None))
    return jax.shard_map(local, mesh=mesh, in_specs=in_specs, out_specs=out_specs, check_vma=False)
```

time: 1400 us -> 70.4 us (0.05); the launches traced: 1380 us -> 70.1 us
  loops' own time: 838 us -> 0 us
  other arithmetic: 213 us -> 0.72 us
  local copies, waits for them, and re-layouts: 210 us -> 4.27 us
  waiting for transfers between devices: 81.3 us -> 28.6 us
  Pallas kernels: 0 us -> 16.2 us
  between operations: 14.9 us -> 0.68 us
    another operation x1 -> x0, loops' own time: 838 us -> none  [legendre_rows(): lax.scan(advance, (empty, empty), jnp.arange(degree_count, dtype=jnp.floa...]
    lt x256 -> x0, other arithmetic: 167 us -> none  [advance(): degree_f < orders_col]
    dynamic_slice x256 -> x1, local copies, waits for them, and re-layouts: 150 us -> 0.61 us  [local(): lax.dynamic_slice_in_dim(row_orders, lax.axis_index('ord') * 8, 8)]
    unnamed x2 -> x0, waiting for transfers between devices: 67.6 us -> none
    reshape x2 -> x1, local copies, waits for them, and re-layouts: 26 us -> 1.22 us  [local(): return (coeffs.reshape(1, 8, 128, 2, 256), potential)]
    all_to_all x4 -> x0, local copies, waits for them, and re-layouts: 24 us -> none  [the longest x1 22.6 us: local(): lax.all_to_all(spectra, 'ord', split_axis=0, concat_axis=1, tiled=True)]
    dynamic_update_slice x256 -> x0, other arithmetic: 22.2 us -> none  [legendre_rows(): lax.scan(advance, (empty, empty), jnp.arange(degree_count, dtype=jnp.floa...]
    pallas_call x0 -> x4, Pallas kernels: none -> 16.2 us  [the longest x1 5.34 us: local(): pl.pallas_call(order_kernel, out_shape=(struct((8, 256, 256), BF16), stru...]
  transfers between devices with their start and end apart: 3 -> 2, of which waited for: 2 -> 2; matrix products, arithmetic and copies ran while one was open for 26% -> 4% of each run, Pallas kernels for 0% -> 7%
where the time goes in v1:
time: 70.4 us; the launch traced here: 70.1 us
  waiting for transfers between devices  28.6 us (41%)
  starting transfers between devices  19.6 us (28%)
  Pallas kernels  16.2 us (23%)
  local copies, waits for them, and re-layouts  4.27 us (6%)
  other arithmetic  0.72 us (1%)
    all_to_all x1, waiting for transfers between devices, local(): lax.all_to_all(modes.reshape(256, 8, 128), ('band', 'ord'), split_axis=0,...  18.7 us
    all_to_all x1, starting transfers between devices, local(): lax.all_to_all(modes.reshape(256, 8, 128), ('band', 'ord'), split_axis=0,...  11 us
    all_to_all x1, waiting for transfers between devices, local(): lax.all_to_all(spectra, 'ord', split_axis=0, concat_axis=0, tiled=True)  9.91 us
    all_to_all x1, starting transfers between devices, local(): lax.all_to_all(spectra, 'ord', split_axis=0, concat_axis=0, tiled=True)  8.58 us
    pallas_call x1, Pallas kernels, local(): pl.pallas_call(order_kernel, out_shape=(struct((8, 256, 256), BF16), stru...  5.34 us
    pallas_call x1, Pallas kernels, local(): pl.pallas_call(table_kernel, out_shape=(struct((8, 256, 256), BF16), stru...  4.98 us
    pallas_call x1, Pallas kernels, local(): pl.pallas_call(forward_kernel, out_shape=struct((32, 128, 128), BF16), in...  3.62 us
    unnamed x8, local copies, waits for them, and re-layouts  2.44 us
  transfers between devices with their start and end apart: 2, of which 2 were waited for; matrix products, arithmetic and copies ran while one was open for 4% of the time, Pallas kernels for 7%

profile of v1, /device:TPU:1, one launch (start us, length us, event | category | flops | bytes accessed | tf_op | source)
XLA Modules:
  0.0 70.1 jit_solution(8825375066106455669)
XLA Ops:
  0.6 3.6 %forward.1 = bf16[32,128,128]{2,1,0:T(8,128)(2,1)} custom-call(s32[1,256]{1,0:T(1,128)} %bitcast.10, bf16[1024,512]{1,0:T(8,128)(2,1)} %bitcast.8, bf16[256,1024]{1,0:T(8,128)(2,1)} %constant.18.clone.table_ref), custom_call_target="tpu_custom_call" | custom-call | tf_op jit(solution)/shard_map/forward/pallas_call | solution.py:193
  4.2 8.6 %all-to-all-start = ((bf16[32,128,128]{2,1,0:T(8,128)(2,1)}), bf16[32,128,128]{2,1,0:T(8,128)(2,1)S(1)}, u32[]{:S(2)}, u32[]{:S(2)}) async-start(bf16[32,128,128]{2,1,0:T(8,128)(2,1)} %forward.1), calls=%async_computation | async-start | bytes 2097152 | tf_op jit(solution)/shard_map/all_to_all | solution.py:201
  12.8 0.0 copy-start.3
  12.8 0.7 copy-done.3
  13.5 0.6 dynamic_slice.3.own_ref
  14.1 0.1 broadcast_multiply_fusion
  14.2 0.1 fusion
  14.2 0.6 pad_maximum_fusion.grid_ref
  14.8 5.0 %tables.1 = (bf16[8,256,256]{2,1,0:T(8,128)(2,1)}, bf16[8,128,256]{2,1,0:T(8,128)(2,1)}, bf16[512,512]{1,0:T(8,128)(2,1)}) custom-call(s32[8]{0:T(128)} %dynamic_slice.3.own_ref, s32[1,256]{1,0:T(1,128)} %bitcast.11, s32[1,128]{1,0:T(1,128)} %bitcast.12, f32[3,256]{1,0:T(4,128)} %pad_maximum_fusion.grid_ref, bf16[256,1024]{1,0:T(8,128)(2,1)} %constant.19.clone.inverse_ref), custom_call_target="tpu_custom_call" | custom-call | tf_op jit(solution)/shard_map/tables/pallas_call | solution.py:203
  19.8 9.9 %all-to-all-done = bf16[32,128,128]{2,1,0:T(8,128)(2,1)S(1)} async-done(((bf16[32,128,128]{2,1,0:T(8,128)(2,1)}), bf16[32,128,128]{2,1,0:T(8,128)(2,1)S(1)}, u32[]{:S(2)}, u32[]{:S(2)}) %all-to-all-start) | async-done | bytes 1048608 | tf_op jit(solution)/shard_map/all_to_all | solution.py:201
  29.7 0.0 copy-start
  29.7 1.0 %copy-done = bf16[32,128,128]{2,1,0:T(8,128)(2,1)} copy-done((bf16[32,128,128]{2,1,0:T(8,128)(2,1)}, bf16[32,128,128]{2,1,0:T(8,128)(2,1)S(1)}, u32[]{:S(2)}) %copy-start) | copy-done | bytes 1048600
  30.7 5.3 %orders.1 = (bf16[8,256,256]{2,1,0:T(8,128)(2,1)}, bf16[2048,128]{1,0:T(8,128)(2,1)}) custom-call(bf16[4096,128]{1,0:T(8,128)(2,1)} %bitcast.6, bf16[8,256,256]{2,1,0:T(8,128)(2,1)} %get-tuple-element.7.analysis_ref, bf16[8,128,256]{2,1,0:T(8,128)(2,1)} %get-tuple-element.8.synthesis_ref, f32[1,256]{1,0:T(1,128)} %weights_ref.1), custom_call_target="tpu_custom_call" | custom-call | tf_op jit(solution)/shard_map/orders/pallas_call | solution.py:216
  36.0 0.0 copy-start.2
  36.0 11.0 %all-to-all-start.1 = ((bf16[256,8,128]{2,1,0:T(8,128)(2,1)}), bf16[256,8,128]{2,1,0:T(8,128)(2,1)S(1)}, u32[]{:S(2)}, u32[]{:S(2)}) async-start(bf16[256,8,128]{2,1,0:T(8,128)(2,1)} %bitcast.9), calls=%async_computation.1 | async-start | bytes 1048576 | tf_op jit(solution)/shard_map/all_to_all | solution.py:225
  47.0 0.0 copy-done.2
  47.1 1.2 %reshape.50 = bf16[1,8,128,2,256]{4,3,2,1,0:T(2,128)(2,1)} reshape(bf16[8,256,256]{2,1,0:T(8,128)(2,1)S(1)} %copy-done.2) | data formatting | bytes 2097152 | tf_op jit(solution)/shard_map/reshape | solution.py:236
  48.3 18.7 %all-to-all-done.1 = bf16[256,8,128]{2,1,0:T(8,128)(2,1)S(1)} async-done(((bf16[256,8,128]{2,1,0:T(8,128)(2,1)}), bf16[256,8,128]{2,1,0:T(8,128)(2,1)S(1)}, u32[]{:S(2)}, u32[]{:S(2)}) %all-to-all-start.1) | async-done | bytes 524320 | tf_op jit(solution)/shard_map/all_to_all | solution.py:225
  67.0 0.0 copy-start.1
  67.0 0.8 %copy-done.1 = bf16[256,8,128]{2,1,0:T(8,128)(2,1)} copy-done((bf16[256,8,128]{2,1,0:T(8,128)(2,1)}, bf16[256,8,128]{2,1,0:T(8,128)(2,1)S(1)}, u32[]{:S(2)}) %copy-start.1) | copy-done | bytes 524312
  67.8 2.3 %inverse.1 = f32[16,4,512]{2,1,0:T(4,128)} custom-call(bf16[2048,128]{1,0:T(8,128)(2,1)} %bitcast.7, bf16[512,512]{1,0:T(8,128)(2,1)} %get-tuple-element.11.inv_ref), custom_call_target="tpu_custom_call" | custom-call | tf_op jit(solution)/shard_map/inverse/pallas_call | solution.py:228
Async XLA Ops:
  4.2 25.5 %all-to-all-start = ((bf16[32,128,128]{2,1,0:T(8,128)(2,1)}), bf16[32,128,128]{2,1,0:T(8,128)(2,1)S(1)}, u32[]{:S(2)}, u32[]{:S(2)}) async-start(bf16[32,128,128]{2,1,0:T(8,128)(2,1)} %forward.1), calls=%async_computation | async-start | bytes 2097152 | tf_op jit(solution)/shard_map/all_to_all | solution.py:201
  12.8 0.7 copy-start.3
  29.7 1.0 %copy-start = (bf16[32,128,128]{2,1,0:T(8,128)(2,1)}, bf16[32,128,128]{2,1,0:T(8,128)(2,1)S(1)}, u32[]{:S(2)}) copy-start(bf16[32,128,128]{2,1,0:T(8,128)(2,1)S(1)} %all-to-all-done) | copy-start | bytes 3145732
  36.0 11.0 %copy-start.2 = (bf16[8,256,256]{2,1,0:T(8,128)(2,1)S(1)}, bf16[8,256,256]{2,1,0:T(8,128)(2,1)}, u32[]{:S(2)}) copy-start(bf16[8,256,256]{2,1,0:T(8,128)(2,1)} %get-tuple-element.9) | copy-start | bytes 3145732
  36.0 30.9 %all-to-all-start.1 = ((bf16[256,8,128]{2,1,0:T(8,128)(2,1)}), bf16[256,8,128]{2,1,0:T(8,128)(2,1)S(1)}, u32[]{:S(2)}, u32[]{:S(2)}) async-start(bf16[256,8,128]{2,1,0:T(8,128)(2,1)} %bitcast.9), calls=%async_computation.1 | async-start | bytes 1048576 | tf_op jit(solution)/shard_map/all_to_all | solution.py:225
  67.0 0.8 %copy-start.1 = (bf16[256,8,128]{2,1,0:T(8,128)(2,1)}, bf16[256,8,128]{2,1,0:T(8,128)(2,1)S(1)}, u32[]{:S(2)}) copy-start(bf16[256,8,128]{2,1,0:T(8,128)(2,1)S(1)} %all-to-all-done.1) | copy-start | bytes 1572868

commit v2 on v1

--- a/solution.py
+++ b/solution.py
@@ -45,26 +45,48 @@
     return one_hot(col == (row % inner) * outer + row // inner)
 
 
-def forward_kernel(orders_ref, density_ref, table_ref, out_ref, turned_ref):
+def forward_kernel(orders_hbm, density_hbm, table_hbm, out_hbm,
+                   orders_ref, density_ref, table_ref, turned_ref, out_ref,
+                   orders_sem, table_sem, density_sem, out_sem):
+    orders_copy = pltpu.make_async_copy(orders_hbm, orders_ref, orders_sem)
+    orders_copy.start()
+    table_copy = pltpu.make_async_copy(table_hbm, table_ref, table_sem)
+    table_copy.start()
+    copies = []
+    for b in range(4):
+        rows = pl.ds(b * 256, 256)
+        copy = pltpu.make_async_copy(density_hbm.at[rows], density_ref.at[rows], density_sem.at[b])
+        copy.start()
+        copies.append(copy)
+    orders_copy.wait()
     picks = one_hot(iota((256, 256), 0) == orders_ref[...])
+    swap = swap_matrix(8, 32)
+    table_copy.wait()
     rows = dot(picks, table_ref[...], TN)
     cos_rows = rows[:, :512].reshape(32, 8, 512)
     sin_rows = rows[:, 512:].reshape(32, 8, 512)
     forward = jnp.stack([cos_rows, sin_rows], axis=1).reshape(512, 512).astype(BF16)
-    swap = swap_matrix(8, 32)
     for b in range(4):
+        copies[b].wait()
         part = dot(swap, density_ref[b * 256 : (b + 1) * 256, :]).astype(BF16)
         turned_ref[:, b * 32 : (b + 1) * 32, :] = part.reshape(8, 32, 512)
+    sends = []
     for j in range(0, 8, 2):
         lanes = turned_ref[j : j + 2].reshape(256, 512)
         part = dot(forward, lanes, NT).astype(BF16)
         for h in range(2):
             block = part[:, h * 128 : (h + 1) * 128].reshape(32, 16, 128)
             out_ref[:, (j + h) * 16 : (j + h + 1) * 16, :] = block
+        rows = pl.ds(j * 16, 32)
+        send = pltpu.make_async_copy(out_ref.at[:, rows], out_hbm.at[:, rows], out_sem.at[j // 2])
+        send.start()
+        sends.append(send)
+    for send in sends:
+        send.wait()
 
 
 def table_kernel(own_ref, orders_ref, target_ref, grid_ref, inverse_ref,
-                 analysis_ref, synthesis_ref, inv_ref, legendre_ref, rows_ref):
+                 legendre_out_ref, inv_ref, legendre_ref, rows_ref):
     sub = iota((8, 256), 0)
     order = jnp.zeros((8, 256), F32)
     for i in range(8):
@@ -118,8 +140,8 @@
     for i in range(8):
         halves = [legendre_ref[h, pl.ds(i, 256, stride=8), :] for h in range(2)]
         own = jnp.concatenate(halves, axis=1)
-        analysis_ref[i] = (own * weights).astype(BF16)
-        synthesis_ref[i] = dot(picks, own.astype(BF16), NT).astype(BF16)
+        legendre_out_ref[i, :256, :] = (own * weights).astype(BF16)
+        legendre_out_ref[i, 256:, :] = dot(picks, own.astype(BF16), NT).astype(BF16)
 
     places = one_hot(iota((256, 256), 0) == orders_ref[...])
     rows = dot(places, inverse_ref[...], TN)
@@ -132,8 +154,9 @@
             inv_ref[top : top + 32, c % 4 * 128 : (c % 4 + 1) * 128] = own
 
 
-def order_kernel(spectra_ref, analysis_ref, synthesis_ref, weights_ref,
-                 coeffs_ref, out_ref, cycles_ref, modes_ref):
+def order_kernel(spectra_ref, legendre_ref, weights_ref,
+                 harmonic_hbm, out_hbm, cycles_ref, modes_ref, harmonic_ref, out_ref,
+                 harmonic_sem, out_sem):
     swap = swap_matrix(16, 16)
     for b in range(0, 16, 2):
         first = spectra_ref[b * 256 : (b + 1) * 256, :]
@@ -144,18 +167,34 @@
     scale = jnp.broadcast_to(weights_ref[...], (128, 256)).T
     scale = jnp.concatenate([scale, scale], axis=1)
     row, col = iota((256, 256), 0), iota((256, 256), 1)
-    interleave = one_hot(col == (row % 2) * 128 + row // 2)
     deal = one_hot(col == (row // 4 % 2) * 128 + row // 8 * 4 + row % 4)
+    sends = []
     for i in range(8):
         lanes = jnp.concatenate([cycles_ref[i], cycles_ref[8 + i]], axis=1)
-        harmonic = dot(analysis_ref[i], lanes).astype(BF16)
-        coeffs_ref[i] = dot(interleave, harmonic, NT).astype(BF16)
+        harmonic = dot(legendre_ref[i, :256, :], lanes).astype(BF16)
+        harmonic_ref[i] = harmonic
+        send = pltpu.make_async_copy(harmonic_ref.at[i], harmonic_hbm.at[i], harmonic_sem.at[i])
+        send.start()
+        sends.append(send)
         scaled = (harmonic.astype(F32) * scale).astype(BF16)
-        modes = dot(synthesis_ref[i], scaled).astype(BF16)
+        modes = dot(legendre_ref[i, 256:, :], scaled).astype(BF16)
         modes_ref[:, i * 16 : (i + 1) * 16, :] = modes.reshape(8, 16, 256)
     for b in range(8):
         block = dot(deal, modes_ref[b], NT)
-        out_ref[b * 256 : (b + 1) * 256, :] = block.astype(BF16)
+        rows = pl.ds(b * 256, 256)
+        out_ref[rows, :] = block.astype(BF16)
+        send = pltpu.make_async_copy(out_ref.at[rows], out_hbm.at[rows], out_sem.at[b])
+        send.start()
+        sends.append(send)
+    for send in sends:
+        send.wait()
+
+
+def coeffs_kernel(harmonic_ref, out_ref):
+    row, col = iota((256, 256), 0), iota((256, 256), 1)
+    interleave = one_hot(col == (row % 2) * 128 + row // 2)
+    for i in range(8):
+        out_ref[i] = dot(interleave, harmonic_ref[i], NT).astype(BF16)
 
 
 def inverse_kernel(modes_ref, inv_ref, out_ref, sum_ref):
@@ -175,12 +214,20 @@
         out_ref[:, q, :] = result[q * 16 : (q + 1) * 16, :]
 
 
-def struct(shape, kind):
-    return jax.ShapeDtypeStruct(shape, kind)
-
-
 VMEM_SPEC = pl.BlockSpec(memory_space=pltpu.VMEM)
 SMEM_SPEC = pl.BlockSpec(memory_space=pltpu.SMEM)
+HBM_SPEC = pl.BlockSpec(memory_space=pltpu.HBM)
+
+
+LIMIT = pltpu.CompilerParams(vmem_limit_bytes=24 << 20)
+
+
+def on_chip(a):
+    return pltpu.with_memory_space_constraint(a, pltpu.VMEM)
+
+
+def off_chip(a):
+    return pltpu.with_memory_space_constraint(a, pltpu.HBM)
 
 
 def local(density, degree_weights, row_orders, target_cycles):
@@ -192,47 +239,75 @@
 
     spectra = pl.pallas_call(
         forward_kernel,
-        out_shape=struct((32, 128, 128), BF16),
-        in_specs=[VMEM_SPEC] * 3,
-        out_specs=VMEM_SPEC,
-        scratch_shapes=[pltpu.VMEM((8, 128, 512), BF16)],
+        out_shape=pltpu.HBM((32, 128, 128), BF16),
+        in_specs=[HBM_SPEC] * 3,
+        out_specs=HBM_SPEC,
+        scratch_shapes=[
+            pltpu.VMEM((1, 256), jnp.int32),
+            pltpu.VMEM((1024, 512), BF16),
+            pltpu.VMEM((256, 1024), BF16),
+            pltpu.VMEM((8, 128, 512), BF16),
+            pltpu.VMEM((32, 128, 128), BF16),
+            pltpu.SemaphoreType.DMA(()),
+            pltpu.SemaphoreType.DMA(()),
+            pltpu.SemaphoreType.DMA((4,)),
+            pltpu.SemaphoreType.DMA((4,)),
+        ],
         name="forward",
-    )(orders_row, density.reshape(1024, 512), jnp.asarray(forward_trig))
+        compiler_params=LIMIT,
+    )(off_chip(orders_row), off_chip(density.reshape(1024, 512)), off_chip(jnp.asarray(forward_trig)))
     by_order = lax.all_to_all(spectra, "ord", split_axis=0, concat_axis=0, tiled=True)
 
-    analysis, synthesis, inverse_rows = pl.pallas_call(
+    legendre, inverse_rows = pl.pallas_call(
         table_kernel,
         out_shape=(
-            struct((8, 256, 256), BF16),
-            struct((8, 128, 256), BF16),
-            struct((512, 512), BF16),
+            pltpu.VMEM((8, 384, 256), BF16),
+            pltpu.HBM((512, 512), BF16),
         ),
         in_specs=[SMEM_SPEC] + [VMEM_SPEC] * 4,
-        out_specs=(VMEM_SPEC,) * 3,
+        out_specs=(VMEM_SPEC,) * 2,
         scratch_shapes=[pltpu.VMEM((2, 2048, 128), F32), pltpu.VMEM((8, 256, 128), F32)],
         name="tables",
+        compiler_params=LIMIT,
     )(own_orders, orders_row, target_cycles.reshape(1, 128), grid, jnp.asarray(inverse_trig))
 
-    coeffs, modes = pl.pallas_call(
+    harmonic, modes = pl.pallas_call(
         order_kernel,
-        out_shape=(struct((8, 256, 256), BF16), struct((2048, 128), BF16)),
-        in_specs=[VMEM_SPEC] * 4,
-        out_specs=(VMEM_SPEC,) * 2,
-        scratch_shapes=[pltpu.VMEM((16, 256, 128), BF16), pltpu.VMEM((8, 128, 256), BF16)],
+        out_shape=(pltpu.HBM((8, 256, 256), BF16), pltpu.HBM((2048, 128), BF16)),
+        in_specs=[VMEM_SPEC] * 3,
+        out_specs=(HBM_SPEC,) * 2,
+        scratch_shapes=[
+            pltpu.VMEM((16, 256, 128), BF16),
+            pltpu.VMEM((8, 128, 256), BF16),
+            pltpu.VMEM((8, 256, 256), BF16),
+            pltpu.VMEM((2048, 128), BF16),
+            pltpu.SemaphoreType.DMA((8,)),
+            pltpu.SemaphoreType.DMA((8,)),
+        ],
         name="orders",
-    )(by_order.reshape(4096, 128), analysis, synthesis, degree_weights)
+        compiler_params=LIMIT,
+    )(on_chip(by_order.reshape(4096, 128)), on_chip(legendre), degree_weights)
 
     arrived = lax.all_to_all(
         modes.reshape(256, 8, 128), ("band", "ord"), split_axis=0, concat_axis=0, tiled=True
     )
+    coeffs = pl.pallas_call(
+        coeffs_kernel,
+        out_shape=pltpu.VMEM((8, 256, 256), BF16),
+        in_specs=[VMEM_SPEC],
+        out_specs=VMEM_SPEC,
+        name="coeffs",
+        compiler_params=LIMIT,
+    )(harmonic)
     potential = pl.pallas_call(
         inverse_kernel,
-        out_shape=struct((16, 4, 512), F32),
+        out_shape=jax.ShapeDtypeStruct((16, 4, 512), F32),
         in_specs=[VMEM_SPEC] * 2,
         out_specs=VMEM_SPEC,
         scratch_shapes=[pltpu.VMEM((256, 128), F32)],
         name="inverse",
-    )(arrived.reshape(2048, 128), inverse_rows)
+        compiler_params=LIMIT,
+    )(on_chip(arrived.reshape(2048, 128)), inverse_rows)
     return coeffs.reshape(1, 8, 128, 2, 256), potential
 
 

time: 70.4 us -> 66.2 us (0.940)
  local copies, waits for them, and re-layouts: 4.27 us -> 1.33 us
  Pallas kernels: 16.2 us -> 13.5 us
  waiting for transfers between devices: 28.6 us -> 30.6 us
    pallas_call x4 -> x5, Pallas kernels: 16.2 us -> 13.5 us  [the longest x1 4.33 us: local(): pl.pallas_call(table_kernel, out_shape=(pltpu.VMEM((8, 384, 256), BF16),...]
    all_to_all x1, waiting for transfers between devices: 9.91 us -> 12.3 us  [local(): lax.all_to_all(spectra, 'ord', split_axis=0, concat_axis=0, tiled=True)]
    unnamed x8 -> x12, local copies, waits for them, and re-layouts: 2.44 us -> 0.04 us
  transfers between devices with their start and end apart: 2 -> 2, of which waited for: 2 -> 2; matrix products, arithmetic and copies ran while one was open for 4% -> 2% of each run, Pallas kernels for 7% -> 7%
where the time goes in v2:
time: 66.2 us; the launch traced here: 66 us
  waiting for transfers between devices  30.6 us (46%)
  starting transfers between devices  19.7 us (30%)
  Pallas kernels  13.5 us (20%)
  local copies, waits for them, and re-layouts  1.33 us (2%)
  between operations  0.77 us (1%)
    all_to_all x1, waiting for transfers between devices, local(): lax.all_to_all(modes.reshape(256, 8, 128), ('band', 'ord'), split_axis=0,...  18.2 us
    all_to_all x1, waiting for transfers between devices, local(): lax.all_to_all(spectra, 'ord', split_axis=0, concat_axis=0, tiled=True)  12.3 us
    all_to_all x1, starting transfers between devices, local(): lax.all_to_all(modes.reshape(256, 8, 128), ('band', 'ord'), split_axis=0,...  11 us
    all_to_all x1, starting transfers between devices, local(): lax.all_to_all(spectra, 'ord', split_axis=0, concat_axis=0, tiled=True)  8.72 us
    pallas_call x1, Pallas kernels, local(): pl.pallas_call(table_kernel, out_shape=(pltpu.VMEM((8, 384, 256), BF16),...  4.33 us
    pallas_call x1, Pallas kernels, local(): pl.pallas_call(forward_kernel, out_shape=pltpu.HBM((32, 128, 128), BF16),...  4.11 us
    pallas_call x1, Pallas kernels, local(): pl.pallas_call(order_kernel, out_shape=(pltpu.HBM((8, 256, 256), BF16), p...  3.49 us
  transfers between devices with their start and end apart: 2, of which 2 were waited for; matrix products, arithmetic and copies ran while one was open for 2% of the time, Pallas kernels for 7%

profile of v2, /device:TPU:1, one launch (start us, length us, event | category | flops | bytes accessed | tf_op | source)
XLA Modules:
  0.0 66.0 jit_solution(16180459732686210078)
XLA Ops:
  0.6 4.1 %forward.1 = bf16[32,128,128]{2,1,0:T(8,128)(2,1)} custom-call(s32[1,256]{1,0:T(1,128)} %bitcast.8, bf16[1024,512]{1,0:T(8,128)(2,1)} %bitcast.11, bf16[256,1024]{1,0:T(8,128)(2,1)} %constant.18.clone.table_hbm), custom_call_target="tpu_custom_call" | custom-call | tf_op jit(solution)/shard_map/forward/pallas_call | solution.py:240
  4.8 0.0 copy-start.3
  4.8 0.0 copy-start.1
  4.8 0.0 copy-start.5
  4.8 0.0 copy-start.4
  4.8 8.7 %all-to-all-start = ((bf16[32,128,128]{2,1,0:T(8,128)(2,1)}), bf16[32,128,128]{2,1,0:T(8,128)(2,1)S(1)}, u32[]{:S(2)}, u32[]{:S(2)}) async-start(bf16[32,128,128]{2,1,0:T(8,128)(2,1)} %forward.1), calls=%async_computation | async-start | bytes 2097152 | tf_op jit(solution)/shard_map/all_to_all | solution.py:259
  13.5 0.0 copy-done.3
  13.5 0.1 dynamic_slice.3.own_ref
  13.6 0.1 broadcast_multiply_fusion
  13.7 0.1 fusion
  13.8 0.0 copy-done.1
  13.8 0.0 copy-done.5
  13.8 4.3 %tables.1 = (bf16[8,384,256]{2,1,0:T(8,128)(2,1)S(1)}, bf16[512,512]{1,0:T(8,128)(2,1)}) custom-call(s32[8]{0:T(128)S(1)} %dynamic_slice.3.own_ref, s32[1,256]{1,0:T(1,128)S(1)} %bitcast.9, s32[1,128]{1,0:T(1,128)S(1)} %bitcast.10, f32[3,256]{1,0:T(4,128)S(1)} %pad_maximum_fusion.grid_ref, bf16[256,1024]{1,0:T(8,128)(2,1)S(1)} %copy-done.1), custom_call_target="tpu_custom_call" | custom-call | tf_op jit(solution)/shard_map/tables/pallas_call | solution.py:261
  18.1 12.3 %all-to-all-done = bf16[32,128,128]{2,1,0:T(8,128)(2,1)S(1)} async-done(((bf16[32,128,128]{2,1,0:T(8,128)(2,1)}), bf16[32,128,128]{2,1,0:T(8,128)(2,1)S(1)}, u32[]{:S(2)}, u32[]{:S(2)}) %all-to-all-start) | async-done | bytes 1048608 | tf_op jit(solution)/shard_map/all_to_all | solution.py:259
  30.4 0.0 copy-done.4
  30.4 3.5 %orders.1 = (bf16[8,256,256]{2,1,0:T(8,128)(2,1)}, bf16[2048,128]{1,0:T(8,128)(2,1)}) custom-call(bf16[4096,128]{1,0:T(8,128)(2,1)S(1)} %bitcast.6, bf16[8,384,256]{2,1,0:T(8,128)(2,1)S(1)} %get-tuple-element.6.legendre_ref, f32[1,256]{1,0:T(1,128)S(1)} %copy-done.4), custom_call_target="tpu_custom_call" | custom-call | tf_op jit(solution)/shard_map/orders/pallas_call | solution.py:274
  33.9 0.0 copy-start
  33.9 11.0 %all-to-all-start.1 = ((bf16[256,8,128]{2,1,0:T(8,128)(2,1)}), bf16[256,8,128]{2,1,0:T(8,128)(2,1)S(1)}, u32[]{:S(2)}, u32[]{:S(2)}) async-start(bf16[256,8,128]{2,1,0:T(8,128)(2,1)} %bitcast.12), calls=%async_computation.1 | async-start | bytes 1048576 | tf_op jit(solution)/shard_map/all_to_all | solution.py:291
  45.0 0.0 copy-done
  45.0 0.5 coeffs.1
  45.5 1.2 %reshape.50 = bf16[1,8,128,2,256]{4,3,2,1,0:T(2,128)(2,1)} reshape(bf16[8,256,256]{2,1,0:T(8,128)(2,1)S(1)} %coeffs.1) | data formatting | bytes 2097152 | tf_op jit(solution)/shard_map/reshape | solution.py:311
  46.7 18.2 %all-to-all-done.1 = bf16[256,8,128]{2,1,0:T(8,128)(2,1)S(1)} async-done(((bf16[256,8,128]{2,1,0:T(8,128)(2,1)}), bf16[256,8,128]{2,1,0:T(8,128)(2,1)S(1)}, u32[]{:S(2)}, u32[]{:S(2)}) %all-to-all-start.1) | async-done | bytes 524320 | tf_op jit(solution)/shard_map/all_to_all | solution.py:291
  64.9 0.0 copy-done.2
  64.9 1.1 %inverse.1 = f32[16,4,512]{2,1,0:T(4,128)} custom-call(bf16[2048,128]{1,0:T(8,128)(2,1)S(1)} %bitcast.7, bf16[512,512]{1,0:T(8,128)(2,1)S(1)} %copy-done.2), custom_call_target="tpu_custom_call" | custom-call | tf_op jit(solution)/shard_map/inverse/pallas_call | solution.py:302
  (2 shorter events, 0.0 us)
Async XLA Ops:
  4.8 8.8 %copy-start.3 = (s32[256]{0:T(256)S(1)}, s32[256]{0:T(256)}, u32[]{:S(2)}) copy-start(s32[256]{0:T(256)} %param.8) | copy-start | bytes 3076
  4.8 9.0 %copy-start.1 = (bf16[256,1024]{1,0:T(8,128)(2,1)S(1)}, bf16[256,1024]{1,0:T(8,128)(2,1)}, u32[]{:S(2)}) copy-start(bf16[256,1024]{1,0:T(8,128)(2,1)} %constant.19.clone.inverse_ref) | copy-start | bytes 1572868
  4.8 9.0 %copy-start.5 = (s32[128]{0:T(128)S(1)}, s32[128]{0:T(128)}, u32[]{:S(2)}) copy-start(s32[128]{0:T(128)} %param.9) | copy-start | bytes 1540
  4.8 25.7 %copy-start.4 = (f32[1,256]{1,0:T(1,128)S(1)}, f32[1,256]{1,0:T(1,128)}, u32[]{:S(2)}) copy-start(f32[1,256]{1,0:T(1,128)} %weights_ref.1) | copy-start | bytes 3076
  4.8 25.6 %all-to-all-start = ((bf16[32,128,128]{2,1,0:T(8,128)(2,1)}), bf16[32,128,128]{2,1,0:T(8,128)(2,1)S(1)}, u32[]{:S(2)}, u32[]{:S(2)}) async-start(bf16[32,128,128]{2,1,0:T(8,128)(2,1)} %forward.1), calls=%async_computation | async-start | bytes 2097152 | tf_op jit(solution)/shard_map/all_to_all | solution.py:259
  33.9 11.0 %copy-start = (bf16[8,256,256]{2,1,0:T(8,128)(2,1)S(1)}, bf16[8,256,256]{2,1,0:T(8,128)(2,1)}, u32[]{:S(2)}) copy-start(bf16[8,256,256]{2,1,0:T(8,128)(2,1)} %get-tuple-element.7.harmonic_ref) | copy-start | bytes 3145732
  33.9 31.0 %all-to-all-start.1 = ((bf16[256,8,128]{2,1,0:T(8,128)(2,1)}), bf16[256,8,128]{2,1,0:T(8,128)(2,1)S(1)}, u32[]{:S(2)}, u32[]{:S(2)}) async-start(bf16[256,8,128]{2,1,0:T(8,128)(2,1)} %bitcast.12), calls=%async_computation.1 | async-start | bytes 1048576 | tf_op jit(solution)/shard_map/all_to_all | solution.py:291
  45.4 19.5 %copy-start.2 = (bf16[512,512]{1,0:T(8,128)(2,1)S(1)}, bf16[512,512]{1,0:T(8,128)(2,1)}, u32[]{:S(2)}) copy-start(bf16[512,512]{1,0:T(8,128)(2,1)} %get-tuple-element.9.inv_ref) | copy-start | bytes 1572868

commit v3 on v2

--- a/solution.py
+++ b/solution.py
@@ -46,28 +46,24 @@
 
 
 def forward_kernel(orders_hbm, density_hbm, table_hbm, out_hbm,
-                   orders_ref, density_ref, table_ref, turned_ref, out_ref,
-                   orders_sem, table_sem, density_sem, out_sem):
-    orders_copy = pltpu.make_async_copy(orders_hbm, orders_ref, orders_sem)
+                   orders_ref, density_ref, table_ref, turned_ref, out_ref, in_sem, out_sem):
+    orders_copy = pltpu.make_async_copy(orders_hbm, orders_ref, in_sem.at[0])
+    table_copy = pltpu.make_async_copy(table_hbm, table_ref, in_sem.at[1])
+    density_copy = pltpu.make_async_copy(density_hbm, density_ref, in_sem.at[2])
     orders_copy.start()
-    table_copy = pltpu.make_async_copy(table_hbm, table_ref, table_sem)
     table_copy.start()
-    copies = []
-    for b in range(4):
-        rows = pl.ds(b * 256, 256)
-        copy = pltpu.make_async_copy(density_hbm.at[rows], density_ref.at[rows], density_sem.at[b])
-        copy.start()
-        copies.append(copy)
+    density_copy.start()
+    swap = swap_matrix(8, 32)
     orders_copy.wait()
-    picks = one_hot(iota((256, 256), 0) == orders_ref[...])
-    swap = swap_matrix(8, 32)
+    hits = jnp.where(iota((256, 256), 0) == orders_ref[...], 1.0, 0.0)
+    picks = hits.T.astype(BF16)
     table_copy.wait()
-    rows = dot(picks, table_ref[...], TN)
+    rows = dot(picks, table_ref[...])
     cos_rows = rows[:, :512].reshape(32, 8, 512)
     sin_rows = rows[:, 512:].reshape(32, 8, 512)
     forward = jnp.stack([cos_rows, sin_rows], axis=1).reshape(512, 512).astype(BF16)
+    density_copy.wait()
     for b in range(4):
-        copies[b].wait()
         part = dot(swap, density_ref[b * 256 : (b + 1) * 256, :]).astype(BF16)
         turned_ref[:, b * 32 : (b + 1) * 32, :] = part.reshape(8, 32, 512)
     sends = []
@@ -77,10 +73,11 @@
         for h in range(2):
             block = part[:, h * 128 : (h + 1) * 128].reshape(32, 16, 128)
             out_ref[:, (j + h) * 16 : (j + h + 1) * 16, :] = block
-        rows = pl.ds(j * 16, 32)
-        send = pltpu.make_async_copy(out_ref.at[:, rows], out_hbm.at[:, rows], out_sem.at[j // 2])
-        send.start()
-        sends.append(send)
+        if j in (2, 6):
+            half = pl.ds((j - 2) * 16, 64)
+            send = pltpu.make_async_copy(out_ref.at[:, half], out_hbm.at[:, half], out_sem.at[j // 4])
+            send.start()
+            sends.append(send)
     for send in sends:
         send.wait()
 
@@ -155,8 +152,7 @@
 
 
 def order_kernel(spectra_ref, legendre_ref, weights_ref,
-                 harmonic_hbm, out_hbm, cycles_ref, modes_ref, harmonic_ref, out_ref,
-                 harmonic_sem, out_sem):
+                 harmonic_hbm, out_hbm, cycles_ref, modes_ref, harmonic_ref, out_ref, out_sem):
     swap = swap_matrix(16, 16)
     for b in range(0, 16, 2):
         first = spectra_ref[b * 256 : (b + 1) * 256, :]
@@ -168,24 +164,25 @@
     scale = jnp.concatenate([scale, scale], axis=1)
     row, col = iota((256, 256), 0), iota((256, 256), 1)
     deal = one_hot(col == (row // 4 % 2) * 128 + row // 8 * 4 + row % 4)
-    sends = []
     for i in range(8):
         lanes = jnp.concatenate([cycles_ref[i], cycles_ref[8 + i]], axis=1)
-        harmonic = dot(legendre_ref[i, :256, :], lanes).astype(BF16)
-        harmonic_ref[i] = harmonic
-        send = pltpu.make_async_copy(harmonic_ref.at[i], harmonic_hbm.at[i], harmonic_sem.at[i])
-        send.start()
-        sends.append(send)
-        scaled = (harmonic.astype(F32) * scale).astype(BF16)
+        harmonic_ref[i] = dot(legendre_ref[i, :256, :], lanes).astype(BF16)
+    for i in range(8):
+        scaled = (harmonic_ref[i].astype(F32) * scale).astype(BF16)
         modes = dot(legendre_ref[i, 256:, :], scaled).astype(BF16)
         modes_ref[:, i * 16 : (i + 1) * 16, :] = modes.reshape(8, 16, 256)
-    for b in range(8):
-        block = dot(deal, modes_ref[b], NT)
-        rows = pl.ds(b * 256, 256)
-        out_ref[rows, :] = block.astype(BF16)
-        send = pltpu.make_async_copy(out_ref.at[rows], out_hbm.at[rows], out_sem.at[b])
-        send.start()
-        sends.append(send)
+    sends = [pltpu.make_async_copy(harmonic_ref, harmonic_hbm, out_sem.at[2])]
+    sends[0].start()
+    for b in range(0, 8, 2):
+        pair = modes_ref[b : b + 2].reshape(256, 256)
+        block = dot(deal, pair, NT).astype(BF16)
+        out_ref[b * 256 : (b + 1) * 256, :] = block[:, :128]
+        out_ref[(b + 1) * 256 : (b + 2) * 256, :] = block[:, 128:]
+        if b in (2, 6):
+            half = pl.ds((b - 2) * 256, 1024)
+            send = pltpu.make_async_copy(out_ref.at[half], out_hbm.at[half], out_sem.at[b // 4])
+            send.start()
+            sends.append(send)
     for send in sends:
         send.wait()
 
@@ -248,10 +245,8 @@
             pltpu.VMEM((256, 1024), BF16),
             pltpu.VMEM((8, 128, 512), BF16),
             pltpu.VMEM((32, 128, 128), BF16),
-            pltpu.SemaphoreType.DMA(()),
-            pltpu.SemaphoreType.DMA(()),
-            pltpu.SemaphoreType.DMA((4,)),
-            pltpu.SemaphoreType.DMA((4,)),
+            pltpu.SemaphoreType.DMA((3,)),
+            pltpu.SemaphoreType.DMA((2,)),
         ],
         name="forward",
         compiler_params=LIMIT,
@@ -281,8 +276,7 @@
             pltpu.VMEM((8, 128, 256), BF16),
             pltpu.VMEM((8, 256, 256), BF16),
             pltpu.VMEM((2048, 128), BF16),
-            pltpu.SemaphoreType.DMA((8,)),
-            pltpu.SemaphoreType.DMA((8,)),
+            pltpu.SemaphoreType.DMA((3,)),
         ],
         name="orders",
         compiler_params=LIMIT,

time: 66.2 us -> 64.1 us (0.968)
  Pallas kernels: 13.5 us -> 11.3 us
    pallas_call x1, Pallas kernels: 3.49 us -> 2.12 us  [local(): pl.pallas_call(order_kernel, out_shape=(pltpu.HBM((8, 256, 256), BF16), p...]
    pallas_call x1, Pallas kernels: 4.11 us -> 3.34 us  [local(): pl.pallas_call(forward_kernel, out_shape=pltpu.HBM((32, 128, 128), BF16),...]
  transfers between devices with their start and end apart: 2 -> 2, of which waited for: 2 -> 2; matrix products, arithmetic and copies ran while one was open for 2% -> 2% of each run, Pallas kernels for 7% -> 8%
where the time goes in v3:
time: 64.1 us; the launch traced here: 63.8 us
  waiting for transfers between devices  30.5 us (48%)
  starting transfers between devices  19.7 us (31%)
  Pallas kernels  11.3 us (18%)
  local copies, waits for them, and re-layouts  1.33 us (2%)
  between operations  0.77 us (1%)
    all_to_all x1, waiting for transfers between devices, local(): lax.all_to_all(modes.reshape(256, 8, 128), ('band', 'ord'), split_axis=0,...  18.2 us
    all_to_all x1, waiting for transfers between devices, local(): lax.all_to_all(spectra, 'ord', split_axis=0, concat_axis=0, tiled=True)  12.3 us
    all_to_all x1, starting transfers between devices, local(): lax.all_to_all(modes.reshape(256, 8, 128), ('band', 'ord'), split_axis=0,...  11 us
    all_to_all x1, starting transfers between devices, local(): lax.all_to_all(spectra, 'ord', split_axis=0, concat_axis=0, tiled=True)  8.72 us
    pallas_call x1, Pallas kernels, local(): pl.pallas_call(table_kernel, out_shape=(pltpu.VMEM((8, 384, 256), BF16),...  4.33 us
    pallas_call x1, Pallas kernels, local(): pl.pallas_call(forward_kernel, out_shape=pltpu.HBM((32, 128, 128), BF16),...  3.34 us
    pallas_call x1, Pallas kernels, local(): pl.pallas_call(order_kernel, out_shape=(pltpu.HBM((8, 256, 256), BF16), p...  2.12 us
  transfers between devices with their start and end apart: 2, of which 2 were waited for; matrix products, arithmetic and copies ran while one was open for 2% of the time, Pallas kernels for 8%

profile of v3, /device:TPU:1, one launch (start us, length us, event | category | flops | bytes accessed | tf_op | source)
XLA Modules:
  0.0 63.8 jit_solution(10969446170681857431)
XLA Ops:
  0.6 3.3 %forward.1 = bf16[32,128,128]{2,1,0:T(8,128)(2,1)} custom-call(s32[1,256]{1,0:T(1,128)} %bitcast.8, bf16[1024,512]{1,0:T(8,128)(2,1)} %bitcast.11, bf16[256,1024]{1,0:T(8,128)(2,1)} %constant.18.clone.table_hbm), custom_call_target="tpu_custom_call" | custom-call | tf_op jit(solution)/shard_map/forward/pallas_call | solution.py:237
  4.0 0.0 copy-start.3
  4.0 0.0 copy-start.1
  4.0 0.0 copy-start.5
  4.0 0.0 copy-start.4
  4.0 8.7 %all-to-all-start = ((bf16[32,128,128]{2,1,0:T(8,128)(2,1)}), bf16[32,128,128]{2,1,0:T(8,128)(2,1)S(1)}, u32[]{:S(2)}, u32[]{:S(2)}) async-start(bf16[32,128,128]{2,1,0:T(8,128)(2,1)} %forward.1), calls=%async_computation | async-start | bytes 2097152 | tf_op jit(solution)/shard_map/all_to_all | solution.py:254
  12.8 0.0 copy-done.3
  12.8 0.1 dynamic_slice.3.own_ref
  12.8 0.1 broadcast_multiply_fusion
  12.9 0.1 fusion
  13.0 0.0 copy-done.1
  13.0 0.0 copy-done.5
  13.0 4.3 %tables.1 = (bf16[8,384,256]{2,1,0:T(8,128)(2,1)S(1)}, bf16[512,512]{1,0:T(8,128)(2,1)}) custom-call(s32[8]{0:T(128)S(1)} %dynamic_slice.3.own_ref, s32[1,256]{1,0:T(1,128)S(1)} %bitcast.9, s32[1,128]{1,0:T(1,128)S(1)} %bitcast.10, f32[3,256]{1,0:T(4,128)S(1)} %pad_maximum_fusion.grid_ref, bf16[256,1024]{1,0:T(8,128)(2,1)S(1)} %copy-done.1), custom_call_target="tpu_custom_call" | custom-call | tf_op jit(solution)/shard_map/tables/pallas_call | solution.py:256
  17.3 12.3 %all-to-all-done = bf16[32,128,128]{2,1,0:T(8,128)(2,1)S(1)} async-done(((bf16[32,128,128]{2,1,0:T(8,128)(2,1)}), bf16[32,128,128]{2,1,0:T(8,128)(2,1)S(1)}, u32[]{:S(2)}, u32[]{:S(2)}) %all-to-all-start) | async-done | bytes 1048608 | tf_op jit(solution)/shard_map/all_to_all | solution.py:254
  29.7 0.0 copy-done.4
  29.7 2.1 %orders.1 = (bf16[8,256,256]{2,1,0:T(8,128)(2,1)}, bf16[2048,128]{1,0:T(8,128)(2,1)}) custom-call(bf16[4096,128]{1,0:T(8,128)(2,1)S(1)} %bitcast.6, bf16[8,384,256]{2,1,0:T(8,128)(2,1)S(1)} %get-tuple-element.6.legendre_ref, f32[1,256]{1,0:T(1,128)S(1)} %copy-done.4), custom_call_target="tpu_custom_call" | custom-call | tf_op jit(solution)/shard_map/orders/pallas_call | solution.py:269
  31.8 0.0 copy-start
  31.8 11.0 %all-to-all-start.1 = ((bf16[256,8,128]{2,1,0:T(8,128)(2,1)}), bf16[256,8,128]{2,1,0:T(8,128)(2,1)S(1)}, u32[]{:S(2)}, u32[]{:S(2)}) async-start(bf16[256,8,128]{2,1,0:T(8,128)(2,1)} %bitcast.12), calls=%async_computation.1 | async-start | bytes 1048576 | tf_op jit(solution)/shard_map/all_to_all | solution.py:285
  42.8 0.0 copy-done
  42.8 0.5 coeffs.1
  43.3 0.0 copy-start.2
  43.3 1.2 %reshape.50 = bf16[1,8,128,2,256]{4,3,2,1,0:T(2,128)(2,1)} reshape(bf16[8,256,256]{2,1,0:T(8,128)(2,1)S(1)} %coeffs.1) | data formatting | bytes 2097152 | tf_op jit(solution)/shard_map/reshape | solution.py:305
  44.5 18.2 %all-to-all-done.1 = bf16[256,8,128]{2,1,0:T(8,128)(2,1)S(1)} async-done(((bf16[256,8,128]{2,1,0:T(8,128)(2,1)}), bf16[256,8,128]{2,1,0:T(8,128)(2,1)S(1)}, u32[]{:S(2)}, u32[]{:S(2)}) %all-to-all-start.1) | async-done | bytes 524320 | tf_op jit(solution)/shard_map/all_to_all | solution.py:285
  62.8 1.1 %inverse.1 = f32[16,4,512]{2,1,0:T(4,128)} custom-call(bf16[2048,128]{1,0:T(8,128)(2,1)S(1)} %bitcast.7, bf16[512,512]{1,0:T(8,128)(2,1)S(1)} %copy-done.2), custom_call_target="tpu_custom_call" | custom-call | tf_op jit(solution)/shard_map/inverse/pallas_call | solution.py:296
  (2 shorter events, 0.0 us)
Async XLA Ops:
  4.0 8.8 %copy-start.3 = (s32[256]{0:T(256)S(1)}, s32[256]{0:T(256)}, u32[]{:S(2)}) copy-start(s32[256]{0:T(256)} %param.8) | copy-start | bytes 3076
  4.0 9.0 %copy-start.1 = (bf16[256,1024]{1,0:T(8,128)(2,1)S(1)}, bf16[256,1024]{1,0:T(8,128)(2,1)}, u32[]{:S(2)}) copy-start(bf16[256,1024]{1,0:T(8,128)(2,1)} %constant.19.clone.inverse_ref) | copy-start | bytes 1572868
  4.0 9.0 %copy-start.5 = (s32[128]{0:T(128)S(1)}, s32[128]{0:T(128)}, u32[]{:S(2)}) copy-start(s32[128]{0:T(128)} %param.9) | copy-start | bytes 1540
  4.0 25.6 %copy-start.4 = (f32[1,256]{1,0:T(1,128)S(1)}, f32[1,256]{1,0:T(1,128)}, u32[]{:S(2)}) copy-start(f32[1,256]{1,0:T(1,128)} %weights_ref.1) | copy-start | bytes 3076
  4.0 25.6 %all-to-all-start = ((bf16[32,128,128]{2,1,0:T(8,128)(2,1)}), bf16[32,128,128]{2,1,0:T(8,128)(2,1)S(1)}, u32[]{:S(2)}, u32[]{:S(2)}) async-start(bf16[32,128,128]{2,1,0:T(8,128)(2,1)} %forward.1), calls=%async_computation | async-start | bytes 2097152 | tf_op jit(solution)/shard_map/all_to_all | solution.py:254
  31.8 11.0 %copy-start = (bf16[8,256,256]{2,1,0:T(8,128)(2,1)S(1)}, bf16[8,256,256]{2,1,0:T(8,128)(2,1)}, u32[]{:S(2)}) copy-start(bf16[8,256,256]{2,1,0:T(8,128)(2,1)} %get-tuple-element.7.harmonic_ref) | copy-start | bytes 3145732
  31.8 31.0 %all-to-all-start.1 = ((bf16[256,8,128]{2,1,0:T(8,128)(2,1)}), bf16[256,8,128]{2,1,0:T(8,128)(2,1)S(1)}, u32[]{:S(2)}, u32[]{:S(2)}) async-start(bf16[256,8,128]{2,1,0:T(8,128)(2,1)} %bitcast.12), calls=%async_computation.1 | async-start | bytes 1048576 | tf_op jit(solution)/shard_map/all_to_all | solution.py:285
  43.3 19.4 %copy-start.2 = (bf16[512,512]{1,0:T(8,128)(2,1)S(1)}, bf16[512,512]{1,0:T(8,128)(2,1)}, u32[]{:S(2)}) copy-start(bf16[512,512]{1,0:T(8,128)(2,1)} %get-tuple-element.9.inv_ref) | copy-start | bytes 1572868

commit v4 on v3

--- a/solution.py
+++ b/solution.py
@@ -82,8 +82,8 @@
         send.wait()
 
 
-def table_kernel(own_ref, orders_ref, target_ref, grid_ref, inverse_ref,
-                 legendre_out_ref, inv_ref, legendre_ref, rows_ref):
+def table_kernel(own_ref, orders_ref, target_ref, grid_ref, inverse_ref, weights_ref,
+                 analysis_ref, transfer_ref, inv_ref, legendre_ref, rows_ref):
     sub = iota((8, 256), 0)
     order = jnp.zeros((8, 256), F32)
     for i in range(8):
@@ -137,8 +137,11 @@
     for i in range(8):
         halves = [legendre_ref[h, pl.ds(i, 256, stride=8), :] for h in range(2)]
         own = jnp.concatenate(halves, axis=1)
-        legendre_out_ref[i, :256, :] = (own * weights).astype(BF16)
-        legendre_out_ref[i, 256:, :] = dot(picks, own.astype(BF16), NT).astype(BF16)
+        analysis = (own * weights).astype(BF16)
+        synthesis = dot(picks, own.astype(BF16), NT)
+        scaled = (synthesis * weights_ref[...]).astype(BF16)
+        analysis_ref[i] = analysis
+        transfer_ref[i] = dot(scaled, analysis).astype(BF16)
 
     places = one_hot(iota((256, 256), 0) == orders_ref[...])
     rows = dot(places, inverse_ref[...], TN)
@@ -151,8 +154,7 @@
             inv_ref[top : top + 32, c % 4 * 128 : (c % 4 + 1) * 128] = own
 
 
-def order_kernel(spectra_ref, legendre_ref, weights_ref,
-                 harmonic_hbm, out_hbm, cycles_ref, modes_ref, harmonic_ref, out_ref, out_sem):
+def turn_cycles(spectra_ref, cycles_ref):
     swap = swap_matrix(16, 16)
     for b in range(0, 16, 2):
         first = spectra_ref[b * 256 : (b + 1) * 256, :]
@@ -160,19 +162,17 @@
         both = dot(swap, jnp.concatenate([first, second], axis=1)).astype(BF16)
         cycles_ref[:, b * 16 : (b + 1) * 16, :] = both[:, :128].reshape(16, 16, 128)
         cycles_ref[:, (b + 1) * 16 : (b + 2) * 16, :] = both[:, 128:].reshape(16, 16, 128)
-    scale = jnp.broadcast_to(weights_ref[...], (128, 256)).T
-    scale = jnp.concatenate([scale, scale], axis=1)
+
+
+def mode_kernel(spectra_ref, transfer_ref, out_hbm, cycles_ref, modes_ref, out_ref, out_sem):
+    turn_cycles(spectra_ref, cycles_ref)
     row, col = iota((256, 256), 0), iota((256, 256), 1)
     deal = one_hot(col == (row // 4 % 2) * 128 + row // 8 * 4 + row % 4)
     for i in range(8):
         lanes = jnp.concatenate([cycles_ref[i], cycles_ref[8 + i]], axis=1)
-        harmonic_ref[i] = dot(legendre_ref[i, :256, :], lanes).astype(BF16)
-    for i in range(8):
-        scaled = (harmonic_ref[i].astype(F32) * scale).astype(BF16)
-        modes = dot(legendre_ref[i, 256:, :], scaled).astype(BF16)
+        modes = dot(transfer_ref[i], lanes).astype(BF16)
         modes_ref[:, i * 16 : (i + 1) * 16, :] = modes.reshape(8, 16, 256)
-    sends = [pltpu.make_async_copy(harmonic_ref, harmonic_hbm, out_sem.at[2])]
-    sends[0].start()
+    sends = []
     for b in range(0, 8, 2):
         pair = modes_ref[b : b + 2].reshape(256, 256)
         block = dot(deal, pair, NT).astype(BF16)
@@ -187,11 +187,14 @@
         send.wait()
 
 
-def coeffs_kernel(harmonic_ref, out_ref):
+def coeffs_kernel(spectra_ref, analysis_ref, out_ref, cycles_ref):
+    turn_cycles(spectra_ref, cycles_ref)
     row, col = iota((256, 256), 0), iota((256, 256), 1)
     interleave = one_hot(col == (row % 2) * 128 + row // 2)
     for i in range(8):
-        out_ref[i] = dot(interleave, harmonic_ref[i], NT).astype(BF16)
+        lanes = jnp.concatenate([cycles_ref[i], cycles_ref[8 + i]], axis=1)
+        harmonic = dot(analysis_ref[i], lanes).astype(BF16)
+        out_ref[i] = dot(interleave, harmonic, NT).astype(BF16)
 
 
 def inverse_kernel(modes_ref, inv_ref, out_ref, sum_ref):
@@ -253,34 +256,36 @@
     )(off_chip(orders_row), off_chip(density.reshape(1024, 512)), off_chip(jnp.asarray(forward_trig)))
     by_order = lax.all_to_all(spectra, "ord", split_axis=0, concat_axis=0, tiled=True)
 
-    legendre, inverse_rows = pl.pallas_call(
+    analysis, transfer, inverse_rows = pl.pallas_call(
         table_kernel,
         out_shape=(
-            pltpu.VMEM((8, 384, 256), BF16),
+            pltpu.HBM((8, 256, 256), BF16),
+            pltpu.VMEM((8, 128, 256), BF16),
             pltpu.HBM((512, 512), BF16),
         ),
-        in_specs=[SMEM_SPEC] + [VMEM_SPEC] * 4,
-        out_specs=(VMEM_SPEC,) * 2,
+        in_specs=[SMEM_SPEC] + [VMEM_SPEC] * 5,
+        out_specs=(VMEM_SPEC,) * 3,
         scratch_shapes=[pltpu.VMEM((2, 2048, 128), F32), pltpu.VMEM((8, 256, 128), F32)],
         name="tables",
         compiler_params=LIMIT,
-    )(own_orders, orders_row, target_cycles.reshape(1, 128), grid, jnp.asarray(inverse_trig))
-
-    harmonic, modes = pl.pallas_call(
-        order_kernel,
-        out_shape=(pltpu.HBM((8, 256, 256), BF16), pltpu.HBM((2048, 128), BF16)),
-        in_specs=[VMEM_SPEC] * 3,
-        out_specs=(HBM_SPEC,) * 2,
+    )(own_orders, orders_row, target_cycles.reshape(1, 128), grid, jnp.asarray(inverse_trig),
+      degree_weights)
+
+    received = on_chip(by_order.reshape(4096, 128))
+    modes = pl.pallas_call(
+        mode_kernel,
+        out_shape=pltpu.HBM((2048, 128), BF16),
+        in_specs=[VMEM_SPEC] * 2,
+        out_specs=HBM_SPEC,
         scratch_shapes=[
             pltpu.VMEM((16, 256, 128), BF16),
             pltpu.VMEM((8, 128, 256), BF16),
-            pltpu.VMEM((8, 256, 256), BF16),
             pltpu.VMEM((2048, 128), BF16),
-            pltpu.SemaphoreType.DMA((3,)),
+            pltpu.SemaphoreType.DMA((2,)),
         ],
-        name="orders",
-        compiler_params=LIMIT,
-    )(on_chip(by_order.reshape(4096, 128)), on_chip(legendre), degree_weights)
+        name="modes",
+        compiler_params=LIMIT,
+    )(received, on_chip(transfer))
 
     arrived = lax.all_to_all(
         modes.reshape(256, 8, 128), ("band", "ord"), split_axis=0, concat_axis=0, tiled=True
@@ -288,11 +293,12 @@
     coeffs = pl.pallas_call(
         coeffs_kernel,
         out_shape=pltpu.VMEM((8, 256, 256), BF16),
-        in_specs=[VMEM_SPEC],
+        in_specs=[VMEM_SPEC] * 2,
         out_specs=VMEM_SPEC,
+        scratch_shapes=[pltpu.VMEM((16, 256, 128), BF16)],
         name="coeffs",
         compiler_params=LIMIT,
-    )(harmonic)
+    )(received, analysis)
     potential = pl.pallas_call(
         inverse_kernel,
         out_shape=jax.ShapeDtypeStruct((16, 4, 512), F32),

time: 64.1 us -> 63.7 us (level)
  waiting for transfers between devices: 30.5 us -> 26 us
  local copies, waits for them, and re-layouts: 1.33 us -> 3.86 us
  Pallas kernels: 11.3 us -> 13 us
    all_to_all x1, waiting for transfers between devices: 12.3 us -> 9.8 us  [local(): lax.all_to_all(spectra, 'ord', split_axis=0, concat_axis=0, tiled=True)]
    unnamed x12, local copies, waits for them, and re-layouts: 0.04 us -> 2.56 us
    all_to_all x1, waiting for transfers between devices: 18.2 us -> 16.2 us  [local(): lax.all_to_all(modes.reshape(256, 8, 128), ('band', 'ord'), split_axis=0,...]
    pallas_call x2, Pallas kernels: 6.45 us -> 7.27 us  [the longest x1 5.53 us: local(): pl.pallas_call(table_kernel, out_shape=(pltpu.HBM((8, 256, 256), BF16), p...]
    pallas_call x1, Pallas kernels: 0.48 us -> 1.27 us  [local(): pl.pallas_call(coeffs_kernel, out_shape=pltpu.VMEM((8, 256, 256), BF16),...]
  transfers between devices with their start and end apart: 2 -> 2, of which waited for: 2 -> 2; matrix products, arithmetic and copies ran while one was open for 2% -> 2% of each run, Pallas kernels for 8% -> 11%
where the time goes in v4:
time: 63.7 us; the launch traced here: 63.4 us
  waiting for transfers between devices  26 us (41%)
  starting transfers between devices  19.7 us (31%)
  Pallas kernels  13 us (20%)
  local copies, waits for them, and re-layouts  3.86 us (6%)
  between operations  0.74 us (1%)
    all_to_all x1, waiting for transfers between devices, local(): lax.all_to_all(modes.reshape(256, 8, 128), ('band', 'ord'), split_axis=0,...  16.2 us
    all_to_all x1, starting transfers between devices, local(): lax.all_to_all(modes.reshape(256, 8, 128), ('band', 'ord'), split_axis=0,...  11 us
    all_to_all x1, waiting for transfers between devices, local(): lax.all_to_all(spectra, 'ord', split_axis=0, concat_axis=0, tiled=True)  9.8 us
    all_to_all x1, starting transfers between devices, local(): lax.all_to_all(spectra, 'ord', split_axis=0, concat_axis=0, tiled=True)  8.72 us
    pallas_call x1, Pallas kernels, local(): pl.pallas_call(table_kernel, out_shape=(pltpu.HBM((8, 256, 256), BF16), p...  5.53 us
    pallas_call x1, Pallas kernels, local(): pl.pallas_call(forward_kernel, out_shape=pltpu.HBM((32, 128, 128), BF16),...  3.34 us
    unnamed x12, local copies, waits for them, and re-layouts  2.56 us
    pallas_call x1, Pallas kernels, local(): pl.pallas_call(mode_kernel, out_shape=pltpu.HBM((2048, 128), BF16), in_sp...  1.74 us
  transfers between devices with their start and end apart: 2, of which 2 were waited for; matrix products, arithmetic and copies ran while one was open for 2% of the time, Pallas kernels for 11%

profile of v4, /device:TPU:1, one launch (start us, length us, event | category | flops | bytes accessed | tf_op | source)
XLA Modules:
  0.0 63.4 jit_solution(9392342096025133534)
XLA Ops:
  0.6 3.3 %forward.1 = bf16[32,128,128]{2,1,0:T(8,128)(2,1)} custom-call(s32[1,256]{1,0:T(1,128)} %bitcast.9, bf16[1024,512]{1,0:T(8,128)(2,1)} %bitcast.13, bf16[256,1024]{1,0:T(8,128)(2,1)} %constant.18.clone.table_hbm), custom_call_target="tpu_custom_call" | custom-call | tf_op jit(solution)/shard_map/forward/pallas_call | solution.py:240
  4.0 0.0 copy-start.1
  4.0 8.7 %all-to-all-start = ((bf16[32,128,128]{2,1,0:T(8,128)(2,1)}), bf16[32,128,128]{2,1,0:T(8,128)(2,1)S(1)}, u32[]{:S(2)}, u32[]{:S(2)}) async-start(bf16[32,128,128]{2,1,0:T(8,128)(2,1)} %forward.1), calls=%async_computation | async-start | bytes 2097152 | tf_op jit(solution)/shard_map/all_to_all | solution.py:257
  12.7 0.0 copy-start.3
  12.7 0.7 %copy-done.3 = s32[256]{0:T(256)S(1)} copy-done((s32[256]{0:T(256)S(1)}, s32[256]{0:T(256)}, u32[]{:S(2)}) %copy-start.3) | copy-done | bytes 1048
  13.4 0.1 dynamic_slice.3.own_ref
  13.5 0.1 broadcast_multiply_fusion
  13.5 0.1 fusion
  13.6 0.0 copy-start.4
  13.6 0.0 copy-start.5
  13.6 0.0 copy-done.1
  13.7 0.6 %copy-done.4 = f32[1,256]{1,0:T(1,128)S(1)} copy-done((f32[1,256]{1,0:T(1,128)S(1)}, f32[1,256]{1,0:T(1,128)}, u32[]{:S(2)}) %copy-start.4) | copy-done | bytes 1048
  14.3 0.0 copy-done.5
  14.3 5.5 %tables.1 = (bf16[8,256,256]{2,1,0:T(8,128)(2,1)}, bf16[8,128,256]{2,1,0:T(8,128)(2,1)S(1)}, bf16[512,512]{1,0:T(8,128)(2,1)}) custom-call(s32[8]{0:T(128)S(1)} %dynamic_slice.3.own_ref, s32[1,256]{1,0:T(1,128)S(1)} %bitcast.10, s32[1,128]{1,0:T(1,128)S(1)} %bitcast.11, f32[3,256]{1,0:T(4,128)S(1)} %pad_maximum_fusion.grid_ref, ...), custom_call_target="tpu_custom_call" | custom-call | tf_op jit(solution)/shard_map/tables/pallas_call | solution.py:259
  19.8 9.8 %all-to-all-done = bf16[32,128,128]{2,1,0:T(8,128)(2,1)S(1)} async-done(((bf16[32,128,128]{2,1,0:T(8,128)(2,1)}), bf16[32,128,128]{2,1,0:T(8,128)(2,1)S(1)}, u32[]{:S(2)}, u32[]{:S(2)}) %all-to-all-start) | async-done | bytes 1048608 | tf_op jit(solution)/shard_map/all_to_all | solution.py:257
  29.6 1.7 %modes.1 = bf16[2048,128]{1,0:T(8,128)(2,1)} custom-call(bf16[4096,128]{1,0:T(8,128)(2,1)S(1)} %bitcast.6, bf16[8,128,256]{2,1,0:T(8,128)(2,1)S(1)} %get-tuple-element.6.transfer_ref), custom_call_target="tpu_custom_call" | custom-call | tf_op jit(solution)/shard_map/modes/pallas_call | solution.py:275
  31.4 11.0 %all-to-all-start.1 = ((bf16[256,8,128]{2,1,0:T(8,128)(2,1)}), bf16[256,8,128]{2,1,0:T(8,128)(2,1)S(1)}, u32[]{:S(2)}, u32[]{:S(2)}) async-start(bf16[256,8,128]{2,1,0:T(8,128)(2,1)} %bitcast.12), calls=%async_computation.1 | async-start | bytes 1048576 | tf_op jit(solution)/shard_map/all_to_all | solution.py:290
  42.4 0.0 copy-start
  42.4 1.2 %copy-done = bf16[8,256,256]{2,1,0:T(8,128)(2,1)S(1)} copy-done((bf16[8,256,256]{2,1,0:T(8,128)(2,1)S(1)}, bf16[8,256,256]{2,1,0:T(8,128)(2,1)}, u32[]{:S(2)}) %copy-start) | copy-done | bytes 1048600
  43.6 1.3 %coeffs.1 = bf16[8,256,256]{2,1,0:T(8,128)(2,1)S(1)} custom-call(bf16[4096,128]{1,0:T(8,128)(2,1)S(1)} %bitcast.7, bf16[8,256,256]{2,1,0:T(8,128)(2,1)S(1)} %copy-done), custom_call_target="tpu_custom_call" | custom-call | tf_op jit(solution)/shard_map/coeffs/pallas_call | solution.py:293
  44.9 0.0 copy-start.2
  44.9 1.2 %reshape.50 = bf16[1,8,128,2,256]{4,3,2,1,0:T(2,128)(2,1)} reshape(bf16[8,256,256]{2,1,0:T(8,128)(2,1)S(1)} %coeffs.1) | data formatting | bytes 2097152 | tf_op jit(solution)/shard_map/reshape | solution.py:311
  46.1 16.2 %all-to-all-done.1 = bf16[256,8,128]{2,1,0:T(8,128)(2,1)S(1)} async-done(((bf16[256,8,128]{2,1,0:T(8,128)(2,1)}), bf16[256,8,128]{2,1,0:T(8,128)(2,1)S(1)}, u32[]{:S(2)}, u32[]{:S(2)}) %all-to-all-start.1) | async-done | bytes 524320 | tf_op jit(solution)/shard_map/all_to_all | solution.py:290
  62.3 1.1 %inverse.1 = f32[16,4,512]{2,1,0:T(4,128)} custom-call(bf16[2048,128]{1,0:T(8,128)(2,1)S(1)} %bitcast.8, bf16[512,512]{1,0:T(8,128)(2,1)S(1)} %copy-done.2), custom_call_target="tpu_custom_call" | custom-call | tf_op jit(solution)/shard_map/inverse/pallas_call | solution.py:302
  (2 shorter events, 0.0 us)
Async XLA Ops:
  4.0 9.7 %copy-start.1 = (bf16[256,1024]{1,0:T(8,128)(2,1)S(1)}, bf16[256,1024]{1,0:T(8,128)(2,1)}, u32[]{:S(2)}) copy-start(bf16[256,1024]{1,0:T(8,128)(2,1)} %constant.19.clone.inverse_ref) | copy-start | bytes 1572868
  4.0 25.6 %all-to-all-start = ((bf16[32,128,128]{2,1,0:T(8,128)(2,1)}), bf16[32,128,128]{2,1,0:T(8,128)(2,1)S(1)}, u32[]{:S(2)}, u32[]{:S(2)}) async-start(bf16[32,128,128]{2,1,0:T(8,128)(2,1)} %forward.1), calls=%async_computation | async-start | bytes 2097152 | tf_op jit(solution)/shard_map/all_to_all | solution.py:257
  12.7 0.7 %copy-start.3 = (s32[256]{0:T(256)S(1)}, s32[256]{0:T(256)}, u32[]{:S(2)}) copy-start(s32[256]{0:T(256)} %param.8) | copy-start | bytes 3076
  13.6 0.7 %copy-start.4 = (f32[1,256]{1,0:T(1,128)S(1)}, f32[1,256]{1,0:T(1,128)}, u32[]{:S(2)}) copy-start(f32[1,256]{1,0:T(1,128)} %weights_ref.1) | copy-start | bytes 3076
  13.6 0.7 %copy-start.5 = (s32[128]{0:T(128)S(1)}, s32[128]{0:T(128)}, u32[]{:S(2)}) copy-start(s32[128]{0:T(128)} %param.9) | copy-start | bytes 1540
  31.4 31.0 %all-to-all-start.1 = ((bf16[256,8,128]{2,1,0:T(8,128)(2,1)}), bf16[256,8,128]{2,1,0:T(8,128)(2,1)S(1)}, u32[]{:S(2)}, u32[]{:S(2)}) async-start(bf16[256,8,128]{2,1,0:T(8,128)(2,1)} %bitcast.12), calls=%async_computation.1 | async-start | bytes 1048576 | tf_op jit(solution)/shard_map/all_to_all | solution.py:290
  42.4 1.2 %copy-start = (bf16[8,256,256]{2,1,0:T(8,128)(2,1)S(1)}, bf16[8,256,256]{2,1,0:T(8,128)(2,1)}, u32[]{:S(2)}) copy-start(bf16[8,256,256]{2,1,0:T(8,128)(2,1)} %get-tuple-element.5.analysis_ref) | copy-start | bytes 3145732
  44.9 17.4 %copy-start.2 = (bf16[512,512]{1,0:T(8,128)(2,1)S(1)}, bf16[512,512]{1,0:T(8,128)(2,1)}, u32[]{:S(2)}) copy-start(bf16[512,512]{1,0:T(8,128)(2,1)} %get-tuple-element.7.inv_ref) | copy-start | bytes 1572868

commit v5 on v4

--- a/solution.py
+++ b/solution.py
@@ -37,6 +37,11 @@
 
 def one_hot(hit):
     return jnp.where(hit, 1.0, 0.0).astype(BF16)
+
+
+def split(a):
+    high = a.astype(BF16)
+    return high, (a - high.astype(F32)).astype(BF16)
 
 
 def swap_matrix(outer, inner):
@@ -139,9 +144,9 @@
         own = jnp.concatenate(halves, axis=1)
         analysis = (own * weights).astype(BF16)
         synthesis = dot(picks, own.astype(BF16), NT)
-        scaled = (synthesis * weights_ref[...]).astype(BF16)
+        high, low = split(synthesis * weights_ref[...])
         analysis_ref[i] = analysis
-        transfer_ref[i] = dot(scaled, analysis).astype(BF16)
+        transfer_ref[i] = (dot(high, analysis) + dot(low, analysis)).astype(BF16)
 
     places = one_hot(iota((256, 256), 0) == orders_ref[...])
     rows = dot(places, inverse_ref[...], TN)
@@ -208,8 +213,9 @@
         turned = jnp.concatenate(parts, axis=0).T
         own = [turned[i * 16 : (i + 1) * 16, :] for i in range(8)]
         blocks.append(jnp.concatenate(own, axis=1))
-    left = jnp.concatenate(blocks, axis=0).astype(BF16)
-    result = dot(left, inv_ref[...])
+    left = jnp.concatenate(split(jnp.concatenate(blocks, axis=0)), axis=0)
+    both = dot(left, inv_ref[...])
+    result = both[:64] + both[64:]
     for q in range(4):
         out_ref[:, q, :] = result[q * 16 : (q + 1) * 16, :]
 

time: 63.7 us -> 63.8 us (level)
    all_to_all x1, waiting for transfers between devices: 9.8 us -> 10.4 us  [local(): lax.all_to_all(spectra, 'ord', split_axis=0, concat_axis=0, tiled=True)]
    pallas_call x1, Pallas kernels: 5.53 us -> 4.88 us  [local(): pl.pallas_call(table_kernel, out_shape=(pltpu.HBM((8, 256, 256), BF16), p...]
  transfers between devices with their start and end apart: 2 -> 2, of which waited for: 2 -> 2; matrix products, arithmetic and copies ran while one was open for 2% -> 2% of each run, Pallas kernels for 11% -> 10%
where the time goes in v5:
time: 63.8 us; the launch traced here: 63.5 us
  waiting for transfers between devices  26.6 us (42%)
  starting transfers between devices  19.7 us (31%)
  Pallas kernels  12.4 us (19%)
  local copies, waits for them, and re-layouts  3.86 us (6%)
  between operations  0.74 us (1%)
    all_to_all x1, waiting for transfers between devices, local(): lax.all_to_all(modes.reshape(256, 8, 128), ('band', 'ord'), split_axis=0,...  16.2 us
    all_to_all x1, starting transfers between devices, local(): lax.all_to_all(modes.reshape(256, 8, 128), ('band', 'ord'), split_axis=0,...  11 us
    all_to_all x1, waiting for transfers between devices, local(): lax.all_to_all(spectra, 'ord', split_axis=0, concat_axis=0, tiled=True)  10.4 us
    all_to_all x1, starting transfers between devices, local(): lax.all_to_all(spectra, 'ord', split_axis=0, concat_axis=0, tiled=True)  8.72 us
    pallas_call x1, Pallas kernels, local(): pl.pallas_call(table_kernel, out_shape=(pltpu.HBM((8, 256, 256), BF16), p...  4.88 us
    pallas_call x1, Pallas kernels, local(): pl.pallas_call(forward_kernel, out_shape=pltpu.HBM((32, 128, 128), BF16),...  3.34 us
    unnamed x12, local copies, waits for them, and re-layouts  2.56 us
    pallas_call x1, Pallas kernels, local(): pl.pallas_call(mode_kernel, out_shape=pltpu.HBM((2048, 128), BF16), in_sp...  1.74 us
  transfers between devices with their start and end apart: 2, of which 2 were waited for; matrix products, arithmetic and copies ran while one was open for 2% of the time, Pallas kernels for 10%

profile of v5, /device:TPU:1, one launch (start us, length us, event | category | flops | bytes accessed | tf_op | source)
XLA Modules:
  0.0 63.5 jit_solution(18327832326639744414)
XLA Ops:
  0.6 3.3 %forward.1 = bf16[32,128,128]{2,1,0:T(8,128)(2,1)} custom-call(s32[1,256]{1,0:T(1,128)} %bitcast.9, bf16[1024,512]{1,0:T(8,128)(2,1)} %bitcast.13, bf16[256,1024]{1,0:T(8,128)(2,1)} %constant.18.clone.table_hbm), custom_call_target="tpu_custom_call" | custom-call | tf_op jit(solution)/shard_map/forward/pallas_call | solution.py:246
  4.0 0.0 copy-start.1
  4.0 8.7 %all-to-all-start = ((bf16[32,128,128]{2,1,0:T(8,128)(2,1)}), bf16[32,128,128]{2,1,0:T(8,128)(2,1)S(1)}, u32[]{:S(2)}, u32[]{:S(2)}) async-start(bf16[32,128,128]{2,1,0:T(8,128)(2,1)} %forward.1), calls=%async_computation | async-start | bytes 2097152 | tf_op jit(solution)/shard_map/all_to_all | solution.py:263
  12.7 0.0 copy-start.3
  12.7 0.7 %copy-done.3 = s32[256]{0:T(256)S(1)} copy-done((s32[256]{0:T(256)S(1)}, s32[256]{0:T(256)}, u32[]{:S(2)}) %copy-start.3) | copy-done | bytes 1048
  13.4 0.1 dynamic_slice.3.own_ref
  13.5 0.1 broadcast_multiply_fusion
  13.5 0.1 fusion
  13.6 0.0 copy-start.4
  13.6 0.0 copy-start.5
  13.6 0.0 copy-done.1
  13.7 0.6 %copy-done.4 = f32[1,256]{1,0:T(1,128)S(1)} copy-done((f32[1,256]{1,0:T(1,128)S(1)}, f32[1,256]{1,0:T(1,128)}, u32[]{:S(2)}) %copy-start.4) | copy-done | bytes 1048
  14.3 0.0 copy-done.5
  14.3 4.9 %tables.1 = (bf16[8,256,256]{2,1,0:T(8,128)(2,1)}, bf16[8,128,256]{2,1,0:T(8,128)(2,1)S(1)}, bf16[512,512]{1,0:T(8,128)(2,1)}) custom-call(s32[8]{0:T(128)S(1)} %dynamic_slice.3.own_ref, s32[1,256]{1,0:T(1,128)S(1)} %bitcast.10, s32[1,128]{1,0:T(1,128)S(1)} %bitcast.11, f32[3,256]{1,0:T(4,128)S(1)} %pad_maximum_fusion.grid_ref, ...), custom_call_target="tpu_custom_call" | custom-call | tf_op jit(solution)/shard_map/tables/pallas_call | solution.py:265
  19.2 10.4 %all-to-all-done = bf16[32,128,128]{2,1,0:T(8,128)(2,1)S(1)} async-done(((bf16[32,128,128]{2,1,0:T(8,128)(2,1)}), bf16[32,128,128]{2,1,0:T(8,128)(2,1)S(1)}, u32[]{:S(2)}, u32[]{:S(2)}) %all-to-all-start) | async-done | bytes 1048608 | tf_op jit(solution)/shard_map/all_to_all | solution.py:263
  29.6 1.7 %modes.1 = bf16[2048,128]{1,0:T(8,128)(2,1)} custom-call(bf16[4096,128]{1,0:T(8,128)(2,1)S(1)} %bitcast.6, bf16[8,128,256]{2,1,0:T(8,128)(2,1)S(1)} %get-tuple-element.6.transfer_ref), custom_call_target="tpu_custom_call" | custom-call | tf_op jit(solution)/shard_map/modes/pallas_call | solution.py:281
  31.4 11.0 %all-to-all-start.1 = ((bf16[256,8,128]{2,1,0:T(8,128)(2,1)}), bf16[256,8,128]{2,1,0:T(8,128)(2,1)S(1)}, u32[]{:S(2)}, u32[]{:S(2)}) async-start(bf16[256,8,128]{2,1,0:T(8,128)(2,1)} %bitcast.12), calls=%async_computation.1 | async-start | bytes 1048576 | tf_op jit(solution)/shard_map/all_to_all | solution.py:296
  42.4 0.0 copy-start
  42.4 1.2 %copy-done = bf16[8,256,256]{2,1,0:T(8,128)(2,1)S(1)} copy-done((bf16[8,256,256]{2,1,0:T(8,128)(2,1)S(1)}, bf16[8,256,256]{2,1,0:T(8,128)(2,1)}, u32[]{:S(2)}) %copy-start) | copy-done | bytes 1048600
  43.6 1.3 %coeffs.1 = bf16[8,256,256]{2,1,0:T(8,128)(2,1)S(1)} custom-call(bf16[4096,128]{1,0:T(8,128)(2,1)S(1)} %bitcast.7, bf16[8,256,256]{2,1,0:T(8,128)(2,1)S(1)} %copy-done), custom_call_target="tpu_custom_call" | custom-call | tf_op jit(solution)/shard_map/coeffs/pallas_call | solution.py:299
  44.9 0.0 copy-start.2
  44.9 1.2 %reshape.50 = bf16[1,8,128,2,256]{4,3,2,1,0:T(2,128)(2,1)} reshape(bf16[8,256,256]{2,1,0:T(8,128)(2,1)S(1)} %coeffs.1) | data formatting | bytes 2097152 | tf_op jit(solution)/shard_map/reshape | solution.py:317
  46.1 16.2 %all-to-all-done.1 = bf16[256,8,128]{2,1,0:T(8,128)(2,1)S(1)} async-done(((bf16[256,8,128]{2,1,0:T(8,128)(2,1)}), bf16[256,8,128]{2,1,0:T(8,128)(2,1)S(1)}, u32[]{:S(2)}, u32[]{:S(2)}) %all-to-all-start.1) | async-done | bytes 524320 | tf_op jit(solution)/shard_map/all_to_all | solution.py:296
  62.3 1.1 %inverse.1 = f32[16,4,512]{2,1,0:T(4,128)} custom-call(bf16[2048,128]{1,0:T(8,128)(2,1)S(1)} %bitcast.8, bf16[512,512]{1,0:T(8,128)(2,1)S(1)} %copy-done.2), custom_call_target="tpu_custom_call" | custom-call | tf_op jit(solution)/shard_map/inverse/pallas_call | solution.py:308
  (2 shorter events, 0.0 us)
Async XLA Ops:
  4.0 9.7 %copy-start.1 = (bf16[256,1024]{1,0:T(8,128)(2,1)S(1)}, bf16[256,1024]{1,0:T(8,128)(2,1)}, u32[]{:S(2)}) copy-start(bf16[256,1024]{1,0:T(8,128)(2,1)} %constant.19.clone.inverse_ref) | copy-start | bytes 1572868
  4.0 25.6 %all-to-all-start = ((bf16[32,128,128]{2,1,0:T(8,128)(2,1)}), bf16[32,128,128]{2,1,0:T(8,128)(2,1)S(1)}, u32[]{:S(2)}, u32[]{:S(2)}) async-start(bf16[32,128,128]{2,1,0:T(8,128)(2,1)} %forward.1), calls=%async_computation | async-start | bytes 2097152 | tf_op jit(solution)/shard_map/all_to_all | solution.py:263
  12.7 0.7 %copy-start.3 = (s32[256]{0:T(256)S(1)}, s32[256]{0:T(256)}, u32[]{:S(2)}) copy-start(s32[256]{0:T(256)} %param.8) | copy-start | bytes 3076
  13.6 0.7 %copy-start.4 = (f32[1,256]{1,0:T(1,128)S(1)}, f32[1,256]{1,0:T(1,128)}, u32[]{:S(2)}) copy-start(f32[1,256]{1,0:T(1,128)} %weights_ref.1) | copy-start | bytes 3076
  13.6 0.7 %copy-start.5 = (s32[128]{0:T(128)S(1)}, s32[128]{0:T(128)}, u32[]{:S(2)}) copy-start(s32[128]{0:T(128)} %param.9) | copy-start | bytes 1540
  31.4 31.0 %all-to-all-start.1 = ((bf16[256,8,128]{2,1,0:T(8,128)(2,1)}), bf16[256,8,128]{2,1,0:T(8,128)(2,1)S(1)}, u32[]{:S(2)}, u32[]{:S(2)}) async-start(bf16[256,8,128]{2,1,0:T(8,128)(2,1)} %bitcast.12), calls=%async_computation.1 | async-start | bytes 1048576 | tf_op jit(solution)/shard_map/all_to_all | solution.py:296
  42.4 1.2 %copy-start = (bf16[8,256,256]{2,1,0:T(8,128)(2,1)S(1)}, bf16[8,256,256]{2,1,0:T(8,128)(2,1)}, u32[]{:S(2)}) copy-start(bf16[8,256,256]{2,1,0:T(8,128)(2,1)} %get-tuple-element.5.analysis_ref) | copy-start | bytes 3145732
  44.9 17.4 %copy-start.2 = (bf16[512,512]{1,0:T(8,128)(2,1)S(1)}, bf16[512,512]{1,0:T(8,128)(2,1)}, u32[]{:S(2)}) copy-start(bf16[512,512]{1,0:T(8,128)(2,1)} %get-tuple-element.7.inv_ref) | copy-start | bytes 1572868

commit v6 on v5

--- a/solution.py
+++ b/solution.py
@@ -51,7 +51,8 @@
 
 
 def forward_kernel(orders_hbm, density_hbm, table_hbm, out_hbm,
-                   orders_ref, density_ref, table_ref, turned_ref, out_ref, in_sem, out_sem):
+                   orders_ref, density_ref, table_ref, turned_ref, stack_ref, out_ref,
+                   in_sem, out_sem):
     orders_copy = pltpu.make_async_copy(orders_hbm, orders_ref, in_sem.at[0])
     table_copy = pltpu.make_async_copy(table_hbm, table_ref, in_sem.at[1])
     density_copy = pltpu.make_async_copy(density_hbm, density_ref, in_sem.at[2])
@@ -72,19 +73,32 @@
         part = dot(swap, density_ref[b * 256 : (b + 1) * 256, :]).astype(BF16)
         turned_ref[:, b * 32 : (b + 1) * 32, :] = part.reshape(8, 32, 512)
     sends = []
-    for j in range(0, 8, 2):
-        lanes = turned_ref[j : j + 2].reshape(256, 512)
-        part = dot(forward, lanes, NT).astype(BF16)
-        for h in range(2):
-            block = part[:, h * 128 : (h + 1) * 128].reshape(32, 16, 128)
-            out_ref[:, (j + h) * 16 : (j + h + 1) * 16, :] = block
-        if j in (2, 6):
-            half = pl.ds((j - 2) * 16, 64)
-            send = pltpu.make_async_copy(out_ref.at[:, half], out_hbm.at[:, half], out_sem.at[j // 4])
-            send.start()
-            sends.append(send)
-    for send in sends:
-        send.wait()
+
+    def finish(half):
+        rows = stack_ref[half * 2048 : (half + 1) * 2048, :].astype(BF16)
+        out_ref[half * 16 : (half + 1) * 16] = rows.reshape(16, 128, 128)
+
+    def send(half):
+        block = pl.ds(half * 16, 16)
+        copy = pltpu.make_async_copy(out_ref.at[block], out_hbm.at[block], out_sem.at[half])
+        copy.start()
+        sends.append(copy)
+
+    for half in range(2):
+        rows = forward[half * 256 : (half + 1) * 256]
+        for j in range(0, 8, 2):
+            lanes = turned_ref[j : j + 2].reshape(256, 512)
+            part = dot(rows, lanes, NT)
+            for e in range(2):
+                places = pl.ds(half * 2048 + j + e, 256, stride=8)
+                stack_ref[places, :] = part[:, e * 128 : (e + 1) * 128]
+            if half == 1 and j == 2:
+                finish(0)
+    send(0)
+    finish(1)
+    send(1)
+    for copy in sends:
+        copy.wait()
 
 
 def table_kernel(own_ref, orders_ref, target_ref, grid_ref, inverse_ref, weights_ref,
@@ -159,23 +173,19 @@
             inv_ref[top : top + 32, c % 4 * 128 : (c % 4 + 1) * 128] = own
 
 
-def turn_cycles(spectra_ref, cycles_ref):
-    swap = swap_matrix(16, 16)
-    for b in range(0, 16, 2):
-        first = spectra_ref[b * 256 : (b + 1) * 256, :]
-        second = spectra_ref[(b + 1) * 256 : (b + 2) * 256, :]
-        both = dot(swap, jnp.concatenate([first, second], axis=1)).astype(BF16)
-        cycles_ref[:, b * 16 : (b + 1) * 16, :] = both[:, :128].reshape(16, 16, 128)
-        cycles_ref[:, (b + 1) * 16 : (b + 2) * 16, :] = both[:, 128:].reshape(16, 16, 128)
-
-
-def mode_kernel(spectra_ref, transfer_ref, out_hbm, cycles_ref, modes_ref, out_ref, out_sem):
-    turn_cycles(spectra_ref, cycles_ref)
+def order_spectra(spectra_ref, i):
+    parts = []
+    for c in range(2):
+        top = (c * 8 + i) * 8
+        parts.append(spectra_ref[:, top : top + 8, :].reshape(256, 128))
+    return jnp.concatenate(parts, axis=1)
+
+
+def mode_kernel(spectra_ref, transfer_ref, out_hbm, modes_ref, out_ref, out_sem):
     row, col = iota((256, 256), 0), iota((256, 256), 1)
     deal = one_hot(col == (row // 4 % 2) * 128 + row // 8 * 4 + row % 4)
     for i in range(8):
-        lanes = jnp.concatenate([cycles_ref[i], cycles_ref[8 + i]], axis=1)
-        modes = dot(transfer_ref[i], lanes).astype(BF16)
+        modes = dot(transfer_ref[i], order_spectra(spectra_ref, i)).astype(BF16)
         modes_ref[:, i * 16 : (i + 1) * 16, :] = modes.reshape(8, 16, 256)
     sends = []
     for b in range(0, 8, 2):
@@ -192,13 +202,11 @@
         send.wait()
 
 
-def coeffs_kernel(spectra_ref, analysis_ref, out_ref, cycles_ref):
-    turn_cycles(spectra_ref, cycles_ref)
+def coeffs_kernel(spectra_ref, analysis_ref, out_ref):
     row, col = iota((256, 256), 0), iota((256, 256), 1)
     interleave = one_hot(col == (row % 2) * 128 + row // 2)
     for i in range(8):
-        lanes = jnp.concatenate([cycles_ref[i], cycles_ref[8 + i]], axis=1)
-        harmonic = dot(analysis_ref[i], lanes).astype(BF16)
+        harmonic = dot(analysis_ref[i], order_spectra(spectra_ref, i)).astype(BF16)
         out_ref[i] = dot(interleave, harmonic, NT).astype(BF16)
 
 
@@ -253,6 +261,7 @@
             pltpu.VMEM((1024, 512), BF16),
             pltpu.VMEM((256, 1024), BF16),
             pltpu.VMEM((8, 128, 512), BF16),
+            pltpu.VMEM((4096, 128), F32),
             pltpu.VMEM((32, 128, 128), BF16),
             pltpu.SemaphoreType.DMA((3,)),
             pltpu.SemaphoreType.DMA((2,)),
@@ -277,14 +286,13 @@
     )(own_orders, orders_row, target_cycles.reshape(1, 128), grid, jnp.asarray(inverse_trig),
       degree_weights)
 
-    received = on_chip(by_order.reshape(4096, 128))
+    received = on_chip(by_order)
     modes = pl.pallas_call(
         mode_kernel,
         out_shape=pltpu.HBM((2048, 128), BF16),
         in_specs=[VMEM_SPEC] * 2,
         out_specs=HBM_SPEC,
         scratch_shapes=[
-            pltpu.VMEM((16, 256, 128), BF16),
             pltpu.VMEM((8, 128, 256), BF16),
             pltpu.VMEM((2048, 128), BF16),
             pltpu.SemaphoreType.DMA((2,)),
@@ -301,7 +309,6 @@
         out_shape=pltpu.VMEM((8, 256, 256), BF16),
         in_specs=[VMEM_SPEC] * 2,
         out_specs=VMEM_SPEC,
-        scratch_shapes=[pltpu.VMEM((16, 256, 128), BF16)],
         name="coeffs",
         compiler_params=LIMIT,
     )(received, analysis)

time: 63.8 us -> 63.6 us (level)
  Pallas kernels: 12.4 us -> 11.7 us
  transfers between devices with their start and end apart: 2 -> 2, of which waited for: 2 -> 2; matrix products, arithmetic and copies ran while one was open for 2% -> 2% of each run, Pallas kernels for 10% -> 9%
where the time goes in v6:
time: 63.6 us; the launch traced here: 63.2 us
  waiting for transfers between devices  27.1 us (43%)
  starting transfers between devices  19.7 us (31%)
  Pallas kernels  11.7 us (18%)
  local copies, waits for them, and re-layouts  3.86 us (6%)
  between operations  0.74 us (1%)
    all_to_all x1, waiting for transfers between devices, local(): lax.all_to_all(modes.reshape(256, 8, 128), ('band', 'ord'), split_axis=0,...  16.6 us
    all_to_all x1, starting transfers between devices, local(): lax.all_to_all(modes.reshape(256, 8, 128), ('band', 'ord'), split_axis=0,...  11 us
    all_to_all x1, waiting for transfers between devices, local(): lax.all_to_all(spectra, 'ord', split_axis=0, concat_axis=0, tiled=True)  10.4 us
    all_to_all x1, starting transfers between devices, local(): lax.all_to_all(spectra, 'ord', split_axis=0, concat_axis=0, tiled=True)  8.72 us
    pallas_call x1, Pallas kernels, local(): pl.pallas_call(table_kernel, out_shape=(pltpu.HBM((8, 256, 256), BF16), p...  4.88 us
    pallas_call x1, Pallas kernels, local(): pl.pallas_call(forward_kernel, out_shape=pltpu.HBM((32, 128, 128), BF16),...  3.48 us
    unnamed x12, local copies, waits for them, and re-layouts  2.56 us
    pallas_call x1, Pallas kernels, local(): pl.pallas_call(mode_kernel, out_shape=pltpu.HBM((2048, 128), BF16), in_sp...  1.35 us
  transfers between devices with their start and end apart: 2, of which 2 were waited for; matrix products, arithmetic and copies ran while one was open for 2% of the time, Pallas kernels for 9%

profile of v6, /device:TPU:1, one launch (start us, length us, event | category | flops | bytes accessed | tf_op | source)
XLA Modules:
  0.0 63.2 jit_solution(15215084576994161002)
XLA Ops:
  0.6 3.5 %forward.1 = bf16[32,128,128]{2,1,0:T(8,128)(2,1)} custom-call(s32[1,256]{1,0:T(1,128)} %bitcast.6, bf16[1024,512]{1,0:T(8,128)(2,1)} %bitcast.10, bf16[256,1024]{1,0:T(8,128)(2,1)} %constant.18.clone.table_hbm), custom_call_target="tpu_custom_call" | custom-call | tf_op jit(solution)/shard_map/forward/pallas_call | solution.py:254
  4.1 0.0 copy-start.1
  4.1 8.7 %all-to-all-start = ((bf16[32,128,128]{2,1,0:T(8,128)(2,1)}), bf16[32,128,128]{2,1,0:T(8,128)(2,1)S(1)}, u32[]{:S(2)}, u32[]{:S(2)}) async-start(bf16[32,128,128]{2,1,0:T(8,128)(2,1)} %forward.1), calls=%async_computation | async-start | bytes 2097152 | tf_op jit(solution)/shard_map/all_to_all | solution.py:272
  12.9 0.0 copy-start.3
  12.9 0.7 %copy-done.3 = s32[256]{0:T(256)S(1)} copy-done((s32[256]{0:T(256)S(1)}, s32[256]{0:T(256)}, u32[]{:S(2)}) %copy-start.3) | copy-done | bytes 1048
  13.5 0.1 dynamic_slice.3.own_ref
  13.6 0.1 broadcast_multiply_fusion
  13.7 0.1 fusion
  13.8 0.0 copy-start.4
  13.8 0.0 copy-start.5
  13.8 0.0 copy-done.1
  13.8 0.6 %copy-done.4 = f32[1,256]{1,0:T(1,128)S(1)} copy-done((f32[1,256]{1,0:T(1,128)S(1)}, f32[1,256]{1,0:T(1,128)}, u32[]{:S(2)}) %copy-start.4) | copy-done | bytes 1048
  14.4 0.0 copy-done.5
  14.4 4.9 %tables.1 = (bf16[8,256,256]{2,1,0:T(8,128)(2,1)}, bf16[8,128,256]{2,1,0:T(8,128)(2,1)S(1)}, bf16[512,512]{1,0:T(8,128)(2,1)}) custom-call(s32[8]{0:T(128)S(1)} %dynamic_slice.3.own_ref, s32[1,256]{1,0:T(1,128)S(1)} %bitcast.7, s32[1,128]{1,0:T(1,128)S(1)} %bitcast.8, f32[3,256]{1,0:T(4,128)S(1)} %pad_maximum_fusion.grid_ref, ...), custom_call_target="tpu_custom_call" | custom-call | tf_op jit(solution)/shard_map/tables/pallas_call | solution.py:274
  19.3 10.4 %all-to-all-done.spectra_ref = bf16[32,128,128]{2,1,0:T(8,128)(2,1)S(1)} async-done(((bf16[32,128,128]{2,1,0:T(8,128)(2,1)}), bf16[32,128,128]{2,1,0:T(8,128)(2,1)S(1)}, u32[]{:S(2)}, u32[]{:S(2)}) %all-to-all-start) | async-done | bytes 1048608 | tf_op jit(solution)/shard_map/all_to_all | solution.py:272
  29.8 1.4 %modes.1 = bf16[2048,128]{1,0:T(8,128)(2,1)} custom-call(bf16[32,128,128]{2,1,0:T(8,128)(2,1)S(1)} %all-to-all-done.spectra_ref, bf16[8,128,256]{2,1,0:T(8,128)(2,1)S(1)} %get-tuple-element.6.transfer_ref), custom_call_target="tpu_custom_call" | custom-call | tf_op jit(solution)/shard_map/modes/pallas_call | solution.py:290
  31.1 11.0 %all-to-all-start.1 = ((bf16[256,8,128]{2,1,0:T(8,128)(2,1)}), bf16[256,8,128]{2,1,0:T(8,128)(2,1)S(1)}, u32[]{:S(2)}, u32[]{:S(2)}) async-start(bf16[256,8,128]{2,1,0:T(8,128)(2,1)} %bitcast.9), calls=%async_computation.1 | async-start | bytes 1048576 | tf_op jit(solution)/shard_map/all_to_all | solution.py:304
  42.1 0.0 copy-start
  42.1 1.2 %copy-done = bf16[8,256,256]{2,1,0:T(8,128)(2,1)S(1)} copy-done((bf16[8,256,256]{2,1,0:T(8,128)(2,1)S(1)}, bf16[8,256,256]{2,1,0:T(8,128)(2,1)}, u32[]{:S(2)}) %copy-start) | copy-done | bytes 1048600
  43.4 0.9 %coeffs.1 = bf16[8,256,256]{2,1,0:T(8,128)(2,1)S(1)} custom-call(bf16[32,128,128]{2,1,0:T(8,128)(2,1)S(1)} %all-to-all-done.spectra_ref, bf16[8,256,256]{2,1,0:T(8,128)(2,1)S(1)} %copy-done), custom_call_target="tpu_custom_call" | custom-call | tf_op jit(solution)/shard_map/coeffs/pallas_call | solution.py:307
  44.2 0.0 copy-start.2
  44.2 1.2 %reshape.46 = bf16[1,8,128,2,256]{4,3,2,1,0:T(2,128)(2,1)} reshape(bf16[8,256,256]{2,1,0:T(8,128)(2,1)S(1)} %coeffs.1) | data formatting | bytes 2097152 | tf_op jit(solution)/shard_map/reshape | solution.py:324
  45.5 16.6 %all-to-all-done.1 = bf16[256,8,128]{2,1,0:T(8,128)(2,1)S(1)} async-done(((bf16[256,8,128]{2,1,0:T(8,128)(2,1)}), bf16[256,8,128]{2,1,0:T(8,128)(2,1)S(1)}, u32[]{:S(2)}, u32[]{:S(2)}) %all-to-all-start.1) | async-done | bytes 524320 | tf_op jit(solution)/shard_map/all_to_all | solution.py:304
  62.1 1.1 %inverse.1 = f32[16,4,512]{2,1,0:T(4,128)} custom-call(bf16[2048,128]{1,0:T(8,128)(2,1)S(1)} %bitcast.5, bf16[512,512]{1,0:T(8,128)(2,1)S(1)} %copy-done.2), custom_call_target="tpu_custom_call" | custom-call | tf_op jit(solution)/shard_map/inverse/pallas_call | solution.py:315
  (2 shorter events, 0.0 us)
Async XLA Ops:
  4.1 9.7 %copy-start.1 = (bf16[256,1024]{1,0:T(8,128)(2,1)S(1)}, bf16[256,1024]{1,0:T(8,128)(2,1)}, u32[]{:S(2)}) copy-start(bf16[256,1024]{1,0:T(8,128)(2,1)} %constant.19.clone.inverse_ref) | copy-start | bytes 1572868
  4.1 25.6 %all-to-all-start = ((bf16[32,128,128]{2,1,0:T(8,128)(2,1)}), bf16[32,128,128]{2,1,0:T(8,128)(2,1)S(1)}, u32[]{:S(2)}, u32[]{:S(2)}) async-start(bf16[32,128,128]{2,1,0:T(8,128)(2,1)} %forward.1), calls=%async_computation | async-start | bytes 2097152 | tf_op jit(solution)/shard_map/all_to_all | solution.py:272
  12.9 0.7 %copy-start.3 = (s32[256]{0:T(256)S(1)}, s32[256]{0:T(256)}, u32[]{:S(2)}) copy-start(s32[256]{0:T(256)} %param.8) | copy-start | bytes 3076
  13.8 0.7 %copy-start.4 = (f32[1,256]{1,0:T(1,128)S(1)}, f32[1,256]{1,0:T(1,128)}, u32[]{:S(2)}) copy-start(f32[1,256]{1,0:T(1,128)} %weights_ref.1) | copy-start | bytes 3076
  13.8 0.7 %copy-start.5 = (s32[128]{0:T(128)S(1)}, s32[128]{0:T(128)}, u32[]{:S(2)}) copy-start(s32[128]{0:T(128)} %param.9) | copy-start | bytes 1540
  31.1 31.0 %all-to-all-start.1 = ((bf16[256,8,128]{2,1,0:T(8,128)(2,1)}), bf16[256,8,128]{2,1,0:T(8,128)(2,1)S(1)}, u32[]{:S(2)}, u32[]{:S(2)}) async-start(bf16[256,8,128]{2,1,0:T(8,128)(2,1)} %bitcast.9), calls=%async_computation.1 | async-start | bytes 1048576 | tf_op jit(solution)/shard_map/all_to_all | solution.py:304
  42.1 1.2 %copy-start = (bf16[8,256,256]{2,1,0:T(8,128)(2,1)S(1)}, bf16[8,256,256]{2,1,0:T(8,128)(2,1)}, u32[]{:S(2)}) copy-start(bf16[8,256,256]{2,1,0:T(8,128)(2,1)} %get-tuple-element.5.analysis_ref) | copy-start | bytes 3145732
  44.2 17.8 %copy-start.2 = (bf16[512,512]{1,0:T(8,128)(2,1)S(1)}, bf16[512,512]{1,0:T(8,128)(2,1)}, u32[]{:S(2)}) copy-start(bf16[512,512]{1,0:T(8,128)(2,1)} %get-tuple-element.7.inv_ref) | copy-start | bytes 1572868
